TPU v7x, 256 devices: a whole 4x4x8 slice. The times are simulated.
256 devices in a mesh: ctx: 64 (over y, z, core), head: 4 (over x).
Axes of the slice: x: 4, y: 4, z: 8, core: 2. Of those that a mesh axis runs over, the one named last changes fastest.
Arguments:
- queries: bfloat16 [65536, 4096], P('ctx', 'head'), may hold values from -6.4 to 6.4
- keys: bfloat16 [65536, 4096], P('ctx', 'head'), may hold values from -0.62 to 0.62
- values: bfloat16 [65536, 4096], P('ctx', 'head'), may hold values from -7.6 to 7.6
- log_decay: float32 [32, 65536], P('head', 'ctx'), may hold values from -1.6 to 0, as said below
- gain: float32 [4096], P('head'), may hold values from 0.1 to 1.9
Outputs:
- shift: float32 [4096], P('head')
- covariance: float32 [4096, 2048], P(('head', 'ctx'))
Inputs may be any that keep to these rules, and one draw needn't show every extreme that they name: log_decay is negative everywhere.
All inputs are finite; a program needn't handle non-finite values.
Results may differ from a plain program's by a relative error of at most 0.0045.
The roundings to bfloat16 on the way count: a program that leaves them out, or rounds other values in their place, can miss the bound.
Values may be sent and summed in bfloat16 or wider, within the bound.
A program may use at most 128 MiB of HBM per device.

v0:
```python
import jax
import jax.numpy as jnp
from jax import lax
from jax.sharding import PartitionSpec as P

HEAD_DIM = 128
SPAN = 256


def entering(value, axis, join, neutral):
    count, mine = (lax.axis_size(axis), lax.axis_index(axis))
    pieces = jax.tree.map(lambda part: lax.all_gather(part, axis), value)
    total = jax.tree.map(
        lambda part, zero: jnp.full_like(part, 0) + jnp.asarray(zero, part.dtype), value, neutral
    )

    def turn(position, total):
        longer = join(total, jax.tree.map(lambda part: part[position], pieces))
        return jax.tree.map(lambda new, old: jnp.where(position < mine, new, old), longer, total)

    return lax.fori_loop(0, count - 1, turn, total)


def merged(value, axis, join):
    pieces = jax.tree.map(lambda part: lax.all_gather(part, axis), value)
    head = jax.tree.map(lambda part: part[0], pieces)
    tail = jax.tree.map(lambda part: part[1:], pieces)
    total, _ = lax.scan(lambda total, slab: (join(total, slab), None), head, tail)
    return total


def from_partner(value, axis, apart):
    mask = 2**apart
    pairs = [(source, source ^ mask) for source in range(lax.axis_size(axis))]
    return lax.ppermute(value, axis, pairs)


def block_step(state, inputs):
    query, key, value, decay = inputs
    cumul = jnp.cumsum(decay, axis=1)
    scores = jnp.einsum("thd,shd->hts", query, key, preferred_element_type=jnp.float32)
    length = query.shape[0]
    later = jnp.arange(length)[:, None] >= jnp.arange(length)[None, :]
    diff = cumul[:, :, None] - cumul[:, None, :]
    factor = jnp.where(later[None], jnp.exp(jnp.where(later[None], diff, 0.0)), 0.0)
    weights = (scores * factor).astype(jnp.bfloat16)
    inner = jnp.einsum("hts,shd->thd", weights, value, preferred_element_type=jnp.float32)
    scaled_q = query.astype(jnp.float32) * jnp.exp(cumul).T[:, :, None]
    outer = jnp.einsum("thd,hde->the", scaled_q, state, precision=lax.Precision.HIGHEST)
    scaled_k = key.astype(jnp.float32) * jnp.exp(cumul[:, -1:] - cumul).T[:, :, None]
    update = jnp.einsum(
        "shd,she->hde", scaled_k, value.astype(jnp.float32), precision=lax.Precision.HIGHEST
    )
    new_state = jnp.exp(cumul[:, -1])[:, None, None] * state + update
    return (new_state, inner + outer)


def run_blocks(start, query, key, value, decay):
    count, heads, size = query.shape
    blocks = count // SPAN
    shaped = (
        query.reshape(blocks, SPAN, heads, size),
        key.reshape(blocks, SPAN, heads, size),
        value.reshape(blocks, SPAN, heads, size),
        decay.reshape(heads, blocks, SPAN).transpose(1, 0, 2),
    )
    ending, raw = lax.scan(block_step, start, shaped)
    return (ending, raw.reshape(count, heads, size))


def chain_join(earlier, later):
    return (earlier[0] * later[0], later[0][:, None, None] * earlier[1] + later[1])


def incoming_state(total, ending):
    heads = total.shape[0]
    identity = (jnp.ones((heads,), jnp.float32), jnp.zeros_like(ending))
    carried = entering((total, ending), "ctx", chain_join, identity)
    return carried[1]


def extreme_join(first, second):
    return (jnp.maximum(first[0], second[0]), jnp.minimum(first[1], second[1]))


def body(queries, keys, values, log_decay, gain):
    count, width = queries.shape
    heads = width // HEAD_DIM
    query = queries.reshape(count, heads, HEAD_DIM)
    key = keys.reshape(count, heads, HEAD_DIM)
    value = values.reshape(count, heads, HEAD_DIM)
    cumul = jnp.cumsum(log_decay, axis=1)
    total = jnp.exp(cumul[:, -1])
    scaled_k = key.astype(jnp.float32) * jnp.exp(cumul[:, -1:] - cumul).T[:, :, None]
    ending = jnp.einsum(
        "shd,she->hde", scaled_k, value.astype(jnp.float32), precision=lax.Precision.HIGHEST
    )
    arrived = incoming_state(total, ending)
    _, raw = run_blocks(arrived, query, key, value, log_decay)
    scale = jnp.sqrt(jnp.mean(raw * raw, axis=-1, keepdims=True) + 1e-06)
    attended = (
        (raw / scale * gain.reshape(heads, HEAD_DIM)).reshape(count, width).astype(jnp.bfloat16)
    )
    top, bottom = merged(
        (jnp.max(attended, axis=0), jnp.min(attended, axis=0)), "ctx", extreme_join
    )
    shift = (top.astype(jnp.float32) + bottom.astype(jnp.float32)) / 2.0
    partner = from_partner(attended, "head", 0)
    own_means = jnp.mean(attended.astype(jnp.float32), axis=0)
    other_means = jnp.mean(partner.astype(jnp.float32), axis=0)
    own_centered = (attended.astype(jnp.float32) - own_means).astype(jnp.bfloat16)
    other_centered = (partner.astype(jnp.float32) - other_means).astype(jnp.bfloat16)
    parity = lax.axis_index("head") % 2
    lower = parity == 0
    pair_data = jnp.concatenate(
        [
            jnp.where(lower, own_centered, other_centered),
            jnp.where(lower, other_centered, own_centered),
        ],
        axis=1,
    )
    pair_means = jnp.concatenate(
        [jnp.where(lower, own_means, other_means), jnp.where(lower, other_means, own_means)]
    )
    offset = parity * width
    shards = lax.axis_size("ctx")
    rows = width // shards
    first_row = lax.axis_index("ctx") * rows
    every_mean = lax.all_gather(pair_means[None, :], "ctx", axis=0, tiled=True)
    channel_spread = every_mean - jnp.mean(every_mean, axis=0)
    spread_rows = lax.dynamic_slice_in_dim(channel_spread, offset + first_row, rows, 1)
    fix = count * jnp.dot(spread_rows.T, channel_spread, precision=lax.Precision.HIGHEST)
    gram = lax.psum_scatter(
        lax.dot_general(
            own_centered, pair_data, (((0,), (0,)), ((), ())), preferred_element_type=jnp.float32
        ),
        "ctx",
        scatter_dimension=0,
        tiled=True,
    )
    covariance = (gram + fix) / (count * shards)
    return (shift, covariance)


def solution(mesh):
    placed = (P("ctx", "head"), P("ctx", "head"), P("ctx", "head"), P("head", "ctx"), P("head"))
    return jax.shard_map(
        body,
        mesh=mesh,
        in_specs=placed,
        out_specs=(P("head"), P(("head", "ctx"), None)),
        check_vma=False,
    )
```

profile of v0, /device:TPU:1, one launch (start us, length us, event | category | flops | bytes accessed | tf_op | source)
XLA Modules:
  0.0 506.1 jit_solution(9900833300421825028)
XLA Ops:
  8.0 2.3 reduce-window.14
  10.9 4.1 copy.83
  15.0 6.1 %fusion.24 = f32[8,128,128]{2,1,0:T(8,128)} fusion(f32[1024,8,128]{0,2,1:T(8,128)} %bitcast.142, f32[1024,8]{0,1:T(8,128)S(1)} %exponential_bitcast_fusion.2, bf16[1024,1024]{1,0:T(8,128)(2,1)} %param.13), kind=kOutput, calls=%fused_computation.51 | convolution fusion | flops 1611661312 | bytes 6848512 | tf_op jit(solution)/shard_map/shd,she->hde/dot_general | solution.py:95
  22.7 132.1 %all-reduce = f32[512]{0:T(512)S(1)} all-reduce(f32[512]{0:T(512)S(1)} %bitcast_dynamic-update-slice_fusion), channel_id=2, replica_groups=mesh['ctx'=64,'head'=4] {'ctx'}, use_global_device_ids=true, to_apply=%add | all-reduce | flops 512 | bytes 4096
  154.9 1.9 copy.92
  156.9 1.9 copy.93
  158.8 2.0 copy.94
  160.8 7.2 %all-gather.7.cloned.1.call-done = f32[512,128,128]{2,1,0:T(8,128)} async-done(((f32[8,128,128]{2,1,0:T(8,128)}), f32[512,128,128]{2,1,0:T(8,128)}) %all-gather.7.cloned.1.call-update) | async-done | bytes 33554448 | tf_op jit(solution)/shard_map/all_gather | solution.py:12
  168.0 76.4 %while.40 = (s32[]{:T(128)}, f32[8,128,128]{2,1,0:T(8,128)S(1)}, s32[]{:T(128)}, f32[64,8]{1,0:T(8,128)S(1)}, f32[64,8,128,128]{3,2,1,0:T(8,128)}, /*index=5*/s32[]{:T(128)}, s32[]{:T(128)}) while((s32[]{:T(128)}, f32[8,128,128]{2,1,0:T(8,128)S(1)}, s32[]{:T(128)}, f32[64,8]{1,0:T(8,128)S(1)}, f32[64,8,128,128]{3,2,1,0:T(8,128)}, ...), condition=%wide.region_3.4_spmd.clone, body=%wide.region_2.3_spmd.clone.sunk | while | flops 524292 | bytes 1573065 | solution.py:21
  244.4 36.9 %while.38 = (s32[]{:T(128)}, f32[8,128,128]{2,1,0:T(8,128)S(1)}, f32[4,256,8,128]{1,3,2,0:T(8,128)}, f32[4,8,256]{2,1,0:T(8,128)}, bf16[4,256,8,128]{3,2,1,0:T(8...) while((s32[]{:T(128)}, f32[8,128,128]{2,1,0:T(8,128)S(1)}, ...), condition=%wide.region_7.8_spmd, body=%wide.region_4.7_spmd.sunk | while | flops 1078265856 | bytes 11248913 | solution.py:67
  249.8 2.0 fusion.44
  252.1 1.6 convolution_add_fusion.2
  259.0 2.0 fusion.44
  261.3 1.6 convolution_add_fusion.2
  268.2 2.0 fusion.44
  270.5 1.6 convolution_add_fusion.2
  277.4 2.0 fusion.44
  279.8 1.6 convolution_add_fusion.2
  281.4 2.6 multiply_reduce_fusion
  284.0 5.3 %copy.78 = f32[4,256,8,128]{3,2,1,0:T(8,128)} copy(f32[4,256,8,128]{1,3,2,0:T(8,128)} %get-tuple-element.162) | data formatting | bytes 8388608 | tf_op jit(solution)/shard_map/while | solution.py:67
  291.6 2.2 fusion.19
  295.3 4.2 convert_reduce_fusion.1
  299.5 41.7 %collective-permute-done = bf16[1024,1024]{1,0:T(8,128)(2,1)} collective-permute-done((bf16[1024,1024]{1,0:T(8,128)(2,1)S(1)}, bf16[1024,1024]{1,0:T(8,128)(2,1)}, u32[]{:S(2)}, u32[]{:S(2)}) %collective-permute-start) | collective-permute-done | bytes 2097184 | tf_op jit(solution)/shard_map/ppermute | solution.py:35
  341.1 2.0 convert_reduce_fusion
  343.1 2.8 broadcast_select_fusion.1
  345.9 7.0 %fusion.20 = f32[1024,2048]{1,0:T(8,128)} fusion(bf16[1024,1024]{1,0:T(8,128)(2,1)S(1)} %get-tuple-element.263, bf16[1024,1024]{1,0:T(8,128)(2,1)S(1)} %get-tuple-element.262, bf16[1024,1024]{1,0:T(8,128)(2,1)S(1)} %fusion.19, f32[1024]{0:T(1024)S(1)} %multiply_bitcast_fusion), kind=kOutput, calls=%fused_computation.43 | convolution fusion | flops 4306501632 | bytes 14684160 | tf_op jit(solution)/shard_map/dot_general | solution.py:134
  352.9 1.6 copy-done.3
  355.3 43.2 %all-gather.4 = bf16[64,1,1024]{2,1,0:T(2,128)(2,1)S(1)} all-gather(bf16[1,1,1024]{2,1,0:T(2,128)(2,1)S(1)} %reshape.171), channel_id=1, replica_groups=mesh['ctx'=64,'head'=4] {'ctx'}, dimensions={0}, use_global_device_ids=true | all-gather | bytes 133120 | tf_op jit(solution)/shard_map/all_gather | solution.py:25
  398.9 43.0 %all-gather.3 = bf16[64,1,1024]{2,1,0:T(2,128)(2,1)S(1)} all-gather(bf16[1,1,1024]{2,1,0:T(2,128)(2,1)S(1)} %reshape.169), channel_id=1, replica_groups=mesh['ctx'=64,'head'=4] {'ctx'}, dimensions={0}, use_global_device_ids=true | all-gather | bytes 133120 | tf_op jit(solution)/shard_map/all_gather | solution.py:25
  442.3 5.5 %while.39 = (s32[]{:T(128)}, bf16[1024]{0:T(1024)(128)(2,1)S(1)}, bf16[1024]{0:T(1024)(128)(2,1)S(1)}, bf16[63,1024]{1,0:T(8,128)(2,1)S(1)}, bf16[63,1024]{1,0:T(8,128)(2,1)S(1)}, /*index=5*/s32[]{:T(128)}) while((s32[]{:T(128)}, bf16[1024]{0:T(1024)(128)(2,1)S(1)}, bf16[1024]{0:T(1024)(128)(2,1)S(1)}, bf16[63,1024]{1,0:T(8,128)(2,1)S(1)}, ...), condition=%wide.region_12.13_spmd, body=%wide.region_11.12_spmd.sunk | while | flops 2050 | bytes 20553 | solution.py:28
  448.4 48.5 %all-gather.2 = f32[131072]{0:T(1024)S(1)} all-gather(f32[2048]{0:T(1024)S(1)} %pad_maximum_fusion), channel_id=4, replica_groups=mesh['ctx'=64,'head'=4] {'ctx'}, dimensions={0}, use_global_device_ids=true | all-gather | bytes 532480 | tf_op jit(solution)/shard_map/all_gather | solution.py:129
  497.7 1.6 add_multiply_fusion
  (421 shorter events, 110.3 us)
Async XLA Ops:
  7.2 160.8 %all-gather.7.cloned.1.call-start = ((), (), s32[]{:S(2)}) async-start(), calls=%async_computation.2 | async-start | bytes 34078720 | tf_op jit(solution)/shard_map/all_gather | solution.py:12
  15.0 6.3 %copy-start.6 = (u32[256]{0:T(256)S(1)}, u32[256]{0:T(256)}, u32[]{:S(2)}) copy-start(u32[256]{0:T(256)} %constant.110) | copy-start | bytes 3076
  15.0 139.9 %copy-start.1 = (bf16[1024,1024]{1,0:T(8,128)(2,1)S(1)}, bf16[1024,1024]{1,0:T(8,128)(2,1)}, u32[]{:S(2)}) copy-start(bf16[1024,1024]{1,0:T(8,128)(2,1)} %param.12) | copy-start | bytes 6291460
  21.2 476.5 %reduce-scatter.2.cloned.1.call-start = ((), (), s32[]{:S(2)}) async-start(), calls=%async_computation.1 | async-start | bytes 8519680 | tf_op jit(solution)/shard_map/reduce_scatter | solution.py:133
  154.9 2.0 copy-start.2
  154.9 3.9 copy-start.4
  289.2 1.4 copy-start.5
  289.4 2.2 copy-start
  293.8 47.3 %collective-permute-start = (bf16[1024,1024]{1,0:T(8,128)(2,1)S(1)}, bf16[1024,1024]{1,0:T(8,128)(2,1)}, u32[]{:S(2)}, u32[]{:S(2)}) collective-permute-start(bf16[1024,1024]{1,0:T(8,128)(2,1)S(1)} %fusion.19), channel_id=1, source_target_pairs={{0,1},{1,0},{2,3},{3,2},{4,5},{5,4},{6,7},{7,6},{8,9},{9,8},{10,11... | collective-permute-start | bytes 6291464 | tf_op jit(solution)/shard_map/ppermute | solution.py:35
  352.9 1.6 copy-start.3
Sparse Core Ops, SparseCore 0:
  21.3 146.6 all-gather.6
  353.0 144.5 reduce-scatter.1
where the time goes:
time: 514 us; the launch traced here: 506 us
  blocking collectives  267 us (52%)
  other arithmetic  98.1 us (19%)
  waiting for transfers between devices  49 us (10%)
  local copies, waits for them, and re-layouts  38.8 us (8%)
  matrix products  33.5 us (7%)
  between operations  14.9 us (3%)
    unnamed x1, blocking collectives  132 us
    all_gather x2, blocking collectives, merged(): pieces = jax.tree.map(lambda part: lax.all_gather(part, axis), value)  86.3 us
    select_n x63, other arithmetic, turn(): jnp.where(position < mine, new, old)  73.9 us
    all_gather x1, blocking collectives, body(): every_mean = lax.all_gather(pair_means[None, :], 'ctx', axis=0, tiled=True)  48.5 us
    ppermute x1, waiting for transfers between devices, from_partner(): return lax.ppermute(value, axis, pairs)  41.7 us
  transfers between devices with their start and end apart: 3, of which 3 were waited for; matrix products, arithmetic and copies ran while one was open for 4% of the time, Pallas kernels for 0%

commit v1 on v0

v1 whole, which is shorter than its diff:
```python
import functools

import jax
import jax.numpy as jnp
from jax import lax
from jax.experimental import pallas as pl
from jax.experimental.pallas import tpu as pltpu
from jax.sharding import PartitionSpec as P

D = 128
SPAN = 256
NZ = 8
NY = 4
F32 = jnp.float32
BF16 = jnp.bfloat16
MESH = pl.DeviceIdType.MESH
TOK = (((0,), (0,)), ((), ()))
LAST = (((1,), (1,)), ((), ()))


def place():
    me = lax.axis_index("ctx")
    core = lax.rem(me, 2)
    z = lax.rem(me // 2, NZ)
    y = me // (2 * NZ)
    return y, z, core


def at(y, z, core):
    return {"ctx": (y * NZ + z) * 2 + core}


def greet(peers):
    barrier = pltpu.get_barrier_semaphore()
    for peer in peers:
        pl.semaphore_signal(barrier, inc=1, device_id=peer, device_id_type=MESH)
    return lambda: pl.semaphore_wait(barrier, len(peers))


def send(src, dst, ssem, rsem, peer):
    copy = pltpu.make_async_remote_copy(
        src_ref=src, dst_ref=dst, send_sem=ssem, recv_sem=rsem, device_id=peer, device_id_type=MESH
    )
    copy.start()
    return copy


def arrived(src, dst, ssem, rsem, peer):
    pltpu.make_async_remote_copy(
        src_ref=src, dst_ref=dst, send_sem=ssem, recv_sem=rsem, device_id=peer, device_id_type=MESH
    ).wait_recv()


def plane_peers(y, z, core):
    peers = [at(y, z, 1 - core)]
    peers += [at(y, lax.rem(z + i, NZ), core) for i in range(1, NZ)]
    peers += [at(lax.rem(y + i, NY), z, core) for i in range(1, NY)]
    return peers


def expand(piece):
    return jnp.concatenate(
        [jnp.broadcast_to(piece[64 + i : 65 + i], (16, D)) for i in range(4)], axis=0
    )


def join(first, second):
    return expand(second) * first[:64] + second[:64], first[64:] * second[64:]


def attend_kernel(
    q_ref, k_ref, v_ref, ld_ref, gain_ref, c_ref, st_ref,
    cum, col, inner, upd, part, other, chip, zin, pre, yin, back, chipin, give, sin,
    s_core, r_core, s_z, r_z, s_y, r_y, s_zb, r_zb, s_cb, r_cb,
):
    y, z, core = place()
    ready = greet(plane_peers(y, z, core))
    mate = at(y, z, 1 - core)

    total = ld_ref[...]
    lane = lax.rem(lax.broadcasted_iota(jnp.int32, total.shape, 1), SPAN)
    step = 1
    while step < SPAN:
        total = total + jnp.where(lane >= step, pltpu.roll(total, step, 1), 0.0)
        step *= 2
    cum[...] = total
    turned = jnp.transpose(total)
    for head in range(8):
        col[head] = jnp.broadcast_to(turned[:, head : head + 1], (4 * SPAN, D))
    part[...] = jnp.zeros_like(part)

    def lanes(head):
        return pl.ds(pl.multiple_of(head * D, D), D)

    def update(head):
        ending = jnp.zeros((D, D), F32)
        decay = jnp.zeros((1, D), F32)
        for b in range(4):
            rows = pl.ds(b * SPAN, SPAN)
            last = col[head, pl.ds(b * SPAN + SPAN - 1, 1), :]
            scaled = v_ref[rows, lanes(head)].astype(F32) * jnp.exp(last - col[head, rows, :])
            high = scaled.astype(BF16)
            low = (scaled - high.astype(F32)).astype(BF16)
            both = lax.dot_general(
                k_ref[rows, lanes(head)],
                jnp.concatenate([high, low], axis=1),
                TOK,
                preferred_element_type=F32,
            )
            new = both[:, :D] + both[:, D:]
            upd[head, b] = new
            ending = jnp.exp(last) * ending + new
            decay = decay + last
        half, local = head // 4, lax.rem(head, 4)
        for owner in range(NZ):
            part[half, owner, pl.ds(pl.multiple_of(local * 16, 16), 16), :] = ending[
                owner * 16 : owner * 16 + 16
            ]
            part[half, owner, pl.ds(64 + local, 1), :] = jnp.exp(decay)

    later = lax.broadcasted_iota(jnp.int32, (SPAN, SPAN), 0) >= lax.broadcasted_iota(
        jnp.int32, (SPAN, SPAN), 1
    )

    def within(head):
        for b in range(4):
            rows = pl.ds(b * SPAN, SPAN)
            value = v_ref[rows, lanes(head)]
            scores = lax.dot_general(
                q_ref[rows, lanes(head)], k_ref[rows, lanes(head)], LAST, preferred_element_type=F32
            )
            mine = col[head, rows, :]
            diff = jnp.concatenate([mine, mine], axis=1) - cum[pl.ds(head, 1), rows]
            weights = jnp.where(later, scores * jnp.exp(jnp.minimum(diff, 0.0)), 0.0)
            inner[head, rows, :] = jnp.dot(weights.astype(BF16), value, preferred_element_type=F32)

    def loop(lo, hi, work, shift=0):
        def turn(i, carry):
            work(lax.rem(i + shift, 8))
            return carry

        lax.fori_loop(lo, hi, turn, 0)

    loop(0, 4, update, 4 * (1 - core))
    ready()
    out = [send(part.at[1 - core], other, s_core, r_core, mate)]
    loop(4, 8, update, 4 * (1 - core))
    loop(0, 1, within)
    out[0].wait_recv()

    def combine(owner, carry):
        mine, theirs = part[core, owner], other[owner]
        first = jnp.where(core == 0, mine, theirs)
        second = jnp.where(core == 0, theirs, mine)
        state, decay = join(first, second)
        chip[owner, :64, :] = state
        chip[owner, 64:, :] = decay
        return carry

    lax.fori_loop(0, NZ, combine, 0)
    for i in range(1, NZ):
        to = lax.rem(z + i, NZ)
        out.append(send(chip.at[to], zin.at[z], s_z.at[i], r_z.at[z], at(y, to, core)))
    zin[z] = chip[z]
    loop(1, 4, within)
    for i in range(1, NZ):
        frm = lax.rem(z + i, NZ)
        arrived(chip.at[frm], zin.at[frm], s_z.at[i], r_z.at[frm], at(y, frm, core))
    state, decay = jnp.zeros((64, D), F32), jnp.ones((8, D), F32)
    for j in range(NZ):
        pre[j, :64, :] = state
        pre[j, 64:, :] = decay
        state, decay = join(jnp.concatenate([state, decay], axis=0), zin[j])
    yin[y, :64, :] = state
    yin[y, 64:, :] = decay
    for i in range(1, NY):
        to = lax.rem(y + i, NY)
        out.append(send(yin.at[y], yin.at[y], s_y.at[i], r_y.at[y], at(to, z, core)))
    loop(4, 5, within)
    for i in range(1, NY):
        frm = lax.rem(y + i, NY)
        arrived(yin.at[frm], yin.at[frm], s_y.at[i], r_y.at[frm], at(frm, z, core))
    row = jnp.zeros((64, D), F32)
    for j in range(NY):
        piece = yin[j]
        row = jnp.where(j < y, expand(piece) * row + piece[:64], row)
    for j in range(NZ):
        piece = pre[j]
        back[j] = expand(piece) * row + piece[:64]
    for i in range(1, NZ):
        to = lax.rem(z + i, NZ)
        out.append(send(back.at[to], chipin.at[z], s_zb.at[i], r_zb.at[z], at(y, to, core)))
    chipin[z] = back[z]
    loop(5, 8, within)
    for i in range(1, NZ):
        frm = lax.rem(z + i, NZ)
        arrived(back.at[frm], chipin.at[frm], s_zb.at[i], r_zb.at[frm], at(y, frm, core))

    def split(owner, carry):
        lead = jnp.where(core == 0, part[core, owner], other[owner])
        early = chipin[owner]
        late = expand(lead) * early + lead[:64]
        give[owner] = jnp.where(core == 0, late, early)
        sin[core, owner] = jnp.where(core == 0, early, late)
        return carry

    lax.fori_loop(0, NZ, split, 0)
    out.append(send(give, sin.at[core], s_cb, r_cb, mate))

    def finish(head):
        half, local = head // 4, lax.rem(head, 4)
        state = jnp.concatenate(
            [sin[half, owner, pl.ds(pl.multiple_of(local * 16, 16), 16), :] for owner in range(NZ)],
            axis=0,
        )
        gain = gain_ref[pl.ds(head, 1), :]
        mean = jnp.zeros((1, D), F32)
        top = bottom = None
        made = []
        for b in range(4):
            rows = pl.ds(b * SPAN, SPAN)
            high = state.astype(BF16)
            low = (state - high.astype(F32)).astype(BF16)
            both = jnp.dot(
                q_ref[rows, lanes(head)],
                jnp.concatenate([high, low], axis=1),
                preferred_element_type=F32,
            )
            raw = inner[head, rows, :] + jnp.exp(col[head, rows, :]) * (both[:, :D] + both[:, D:])
            scale = jnp.sqrt(jnp.mean(raw * raw, axis=1, keepdims=True) + 1e-06)
            done = (raw / scale * gain).astype(BF16).astype(F32)
            mean = mean + jnp.sum(done, axis=0, keepdims=True)
            high_b = jnp.max(done, axis=0, keepdims=True)
            low_b = jnp.min(done, axis=0, keepdims=True)
            top = high_b if top is None else jnp.maximum(top, high_b)
            bottom = low_b if bottom is None else jnp.minimum(bottom, low_b)
            made.append(done)
            inner[head, rows, :] = done
            if b < 3:
                last = col[head, pl.ds(b * SPAN + SPAN - 1, 1), :]
                state = jnp.exp(last) * state + upd[head, b]
        mean = mean / (4 * SPAN)
        for b in range(4):
            rows = pl.ds(b * SPAN, SPAN)
            c_ref[rows, lanes(head)] = (inner[head, rows, :] - mean).astype(BF16)
        st_ref[pl.ds(head, 1), :] = mean
        st_ref[pl.ds(8 + head, 1), :] = top
        st_ref[pl.ds(16 + head, 1), :] = bottom

    loop(0, 4, finish, 4 * core)
    out[-1].wait_recv()
    loop(4, 8, finish, 4 * core)
    for copy in out:
        copy.wait_send()


def attend(q, k, v, log_decay, gain):
    count, width = q.shape
    vm = pl.BlockSpec(memory_space=pltpu.VMEM)
    dma = pltpu.SemaphoreType.DMA
    return pl.pallas_call(
        attend_kernel,
        out_shape=(
            jax.ShapeDtypeStruct((count, width), BF16),
            jax.ShapeDtypeStruct((24, D), F32),
        ),
        in_specs=[vm] * 5,
        out_specs=(vm, vm),
        scratch_shapes=[
            pltpu.VMEM((8, 1024), F32),
            pltpu.VMEM((8, 1024, D), F32),
            pltpu.VMEM((8, 1024, D), F32),
            pltpu.VMEM((8, 4, D, D), F32),
            pltpu.VMEM((2, NZ, 72, D), F32),
            pltpu.VMEM((NZ, 72, D), F32),
            pltpu.VMEM((NZ, 72, D), F32),
            pltpu.VMEM((NZ, 72, D), F32),
            pltpu.VMEM((NZ, 72, D), F32),
            pltpu.VMEM((NY, 72, D), F32),
            pltpu.VMEM((NZ, 64, D), F32),
            pltpu.VMEM((NZ, 64, D), F32),
            pltpu.VMEM((NZ, 64, D), F32),
            pltpu.VMEM((2, NZ, 64, D), F32),
            dma, dma, dma((NZ,)), dma((NZ,)), dma((NY,)), dma((NY,)), dma((NZ,)), dma((NZ,)), dma, dma,
        ],
        compiler_params=pltpu.CompilerParams(
            collective_id=0, has_side_effects=True, vmem_limit_bytes=60 * 1024 * 1024
        ),
        name="attend",
    )(q, k, v, log_decay, gain.reshape(8, D))


def gram_kernel(
    c_ref, st_ref, shift_ref, cov_ref,
    theirs, full, grams, mates, sums, ylow, yhigh, ylast, yfirst, ynext, yprev, zsend, zin, strip, hop,
    st1, stsum, stz, sty, off, offin,
    s_x, r_x, s_c, r_c, s_y1, r_y1, s_y2, r_y2, s_z, r_z, s_h, r_h, s_s1, r_s1, s_sz, r_sz, s_sy, r_sy, s_o, r_o,
):
    y, z, core = place()
    parity = lax.rem(lax.axis_index("head"), 2)
    pair = {"head": lax.axis_index("head") + 1 - 2 * parity}
    mate = at(y, z, 1 - core)
    north, south = lax.rem(y + 1, NY), lax.rem(y + NY - 1, NY)
    far = lax.rem(y + 2, NY)
    ready = greet(plane_peers(y, z, core) + [pair])
    ready()
    out = []

    def keep(copy):
        out.append(copy)
        return copy

    other_half = pl.ds(pl.multiple_of((1 - parity) * 512, 512), 512)
    half = pl.ds(pl.multiple_of(parity * 512, 512), 512)
    swap = keep(send(c_ref.at[other_half], theirs, s_x, r_x, pair))
    first = keep(send(st_ref, st1, s_s1, r_s1, mate))

    def diagonal(i):
        full[pl.ds(i * 256, 256), :] = lax.dot_general(
            c_ref[:, i * 256 : i * 256 + 256], c_ref[...], TOK, preferred_element_type=F32
        )

    def merge(a, b):
        return jnp.concatenate(
            [a[:8] + b[:8], jnp.maximum(a[8:16], b[8:16]), jnp.minimum(a[16:], b[16:])], axis=0
        )

    diagonal(0)
    first.wait_recv()
    stz[z] = merge(st_ref[...], st1[...])
    for i in range(1, NZ):
        to = lax.rem(z + i, NZ)
        keep(send(stz.at[z], stz.at[z], s_sz.at[i], r_sz.at[z], at(y, to, core)))
    diagonal(1)
    diagonal(2)
    for i in range(1, NZ):
        frm = lax.rem(z + i, NZ)
        arrived(stz.at[frm], stz.at[frm], s_sz.at[i], r_sz.at[frm], at(y, frm, core))
    sty[y] = functools.reduce(merge, [stz[j] for j in range(NZ)])
    for i in range(1, NY):
        to = lax.rem(y + i, NY)
        keep(send(sty.at[y], sty.at[y], s_sy.at[i], r_sy.at[y], at(to, z, core)))
    diagonal(3)
    for i in range(1, NY):
        frm = lax.rem(y + i, NY)
        arrived(sty.at[frm], sty.at[frm], s_sy.at[i], r_sy.at[frm], at(frm, z, core))
    every = functools.reduce(merge, [sty[j] for j in range(NY)])
    shift_ref[...] = (every[8:16] + every[16:]) / 2.0
    off[...] = st_ref[:8, :] - every[:8] / 64.0
    offset = keep(send(off, offin, s_o, r_o, pair))

    def spread(tall, wide, weight, i):
        column = jnp.transpose(tall)
        rows = [
            jnp.concatenate(
                [
                    weight * jnp.broadcast_to(column[:, h : h + 1], (D, D)) * wide[j : j + 1, :]
                    for j in range(8)
                ],
                axis=1,
            )
            for h in (2 * i, 2 * i + 1)
        ]
        return jnp.concatenate(rows, axis=0)

    def store(seg, i, value):
        grams[seg, pl.ds(8 * i, 8)] = value.astype(BF16).reshape(8, 2, 16, 1024)

    mine = off[...]
    for i in range(4):
        store(0, i, full[pl.ds(i * 256, 256), :] + spread(mine, mine, 1024.0, i))

    def to_mate(seg):
        return keep(send(grams.at[seg, :, 1 - core], mates.at[seg], s_c.at[seg], r_c.at[seg], mate))

    def add_mate(seg, copy):
        copy.wait_recv()

        def turn(i, carry):
            got = grams[seg, i, core].astype(F32) + mates[seg, i].astype(F32)
            sums[seg, i // NZ, lax.rem(i, NZ)] = got.astype(BF16)
            return carry

        lax.fori_loop(0, NZ * NY, turn, 0)
        up = keep(
            send(sums.at[seg, far, :, :, pl.ds(0, 512)], ylow.at[seg], s_y1.at[seg, 0], r_y1.at[seg, 0], at(north, z, core))
        )
        down = keep(
            send(sums.at[seg, far, :, :, pl.ds(512, 512)], yhigh.at[seg], s_y1.at[seg, 1], r_y1.at[seg, 1], at(south, z, core))
        )
        return up, down

    def pass_on(seg, copies):
        copies[0].wait_recv()
        copies[1].wait_recv()

        def turn(i, carry):
            a, b = sums[seg, north, i].astype(F32), sums[seg, south, i].astype(F32)
            low, high = ylow[seg, i].astype(F32), yhigh[seg, i].astype(F32)
            ynext[seg, i] = jnp.concatenate([a[:, :512] + low, a[:, 512:]], axis=1).astype(BF16)
            yprev[seg, i] = jnp.concatenate([b[:, :512], b[:, 512:] + high], axis=1).astype(BF16)
            return carry

        lax.fori_loop(0, NZ, turn, 0)
        up = keep(send(ynext.at[seg], yfirst.at[seg], s_y2.at[seg, 0], r_y2.at[seg, 0], at(north, z, core)))
        down = keep(send(yprev.at[seg], ylast.at[seg], s_y2.at[seg, 1], r_y2.at[seg, 1], at(south, z, core)))
        return up, down

    def to_z(seg, copies):
        copies[0].wait_recv()
        copies[1].wait_recv()

        def turn(i, carry):
            got = sums[seg, y, i].astype(F32) + yfirst[seg, i].astype(F32) + ylast[seg, i].astype(F32)
            zsend[seg, i] = got.astype(BF16)
            return carry

        lax.fori_loop(0, NZ, turn, 0)
        for i in range(1, NZ):
            to = lax.rem(z + i, NZ)
            keep(
                send(zsend.at[seg, to], zin.at[seg, z], s_z.at[seg, i], r_z.at[seg, z], at(y, to, core))
            )
        zin[seg, z] = zsend[seg, z]

    def from_z(seg):
        for i in range(1, NZ):
            frm = lax.rem(z + i, NZ)
            arrived(
                zsend.at[seg, frm], zin.at[seg, frm], s_z.at[seg, i], r_z.at[seg, frm], at(y, frm, core)
            )
        got = zin[seg, 0].astype(F32)
        for j in range(1, NZ):
            got = got + zin[seg, j].astype(F32)
        return got

    core0 = to_mate(0)
    ph1 = add_mate(0, core0)
    ph2 = pass_on(0, ph1)
    offset.wait_recv()
    swap.wait_recv()
    pairs = offin[...]
    for i in range(4):
        value = lax.dot_general(
            theirs[:, i * 256 : i * 256 + 256], c_ref[half, :], TOK, preferred_element_type=F32
        )
        store(1, i, value + spread(pairs, mine, 512.0, i))
    core1 = to_mate(1)
    for i in range(4):
        value = lax.dot_general(
            c_ref[half, i * 256 : i * 256 + 256], theirs[...], TOK, preferred_element_type=F32
        )
        store(2, i, value + spread(mine, pairs, 512.0, i))
    core2 = to_mate(2)
    to_z(0, ph2)
    ph1a = add_mate(1, core1)
    ph1b = add_mate(2, core2)
    ph2a = pass_on(1, ph1a)
    diag = from_z(0)
    ph2b = pass_on(2, ph1b)
    to_z(1, ph2a)
    to_z(2, ph2b)
    strip[...] = from_z(1)
    final = keep(send(strip, hop, s_h, r_h, pair))
    cross = from_z(2)
    final.wait_recv()
    cross = (cross + hop[...]) / 65536.0
    diag = diag / 65536.0
    cov_ref[:, :1024] = jnp.where(parity == 0, diag, cross)
    cov_ref[:, 1024:] = jnp.where(parity == 0, cross, diag)
    for copy in out:
        copy.wait_send()


def gram(centered, stats):
    vm = pl.BlockSpec(memory_space=pltpu.VMEM)
    dma = pltpu.SemaphoreType.DMA
    return pl.pallas_call(
        gram_kernel,
        out_shape=(
            jax.ShapeDtypeStruct((8, D), F32),
            jax.ShapeDtypeStruct((16, 2048), F32),
        ),
        in_specs=[vm] * 2,
        out_specs=(vm, vm),
        scratch_shapes=[
            pltpu.VMEM((512, 1024), BF16),
            pltpu.VMEM((1024, 1024), F32),
            pltpu.VMEM((3, 32, 2, 16, 1024), BF16),
            pltpu.VMEM((3, 32, 16, 1024), BF16),
            pltpu.VMEM((3, NY, NZ, 16, 1024), BF16),
            pltpu.VMEM((3, NZ, 16, 512), BF16),
            pltpu.VMEM((3, NZ, 16, 512), BF16),
            pltpu.VMEM((3, NZ, 16, 1024), BF16),
            pltpu.VMEM((3, NZ, 16, 1024), BF16),
            pltpu.VMEM((3, NZ, 16, 1024), BF16),
            pltpu.VMEM((3, NZ, 16, 1024), BF16),
            pltpu.VMEM((3, NZ, 16, 1024), BF16),
            pltpu.VMEM((3, NZ, 16, 1024), BF16),
            pltpu.VMEM((16, 1024), F32),
            pltpu.VMEM((16, 1024), F32),
            pltpu.VMEM((24, D), F32),
            pltpu.VMEM((24, D), F32),
            pltpu.VMEM((NZ, 24, D), F32),
            pltpu.VMEM((NY, 24, D), F32),
            pltpu.VMEM((8, D), F32),
            pltpu.VMEM((8, D), F32),
            dma, dma, dma((3,)), dma((3,)), dma((3, 2)), dma((3, 2)), dma((3, 2)), dma((3, 2)),
            dma((3, NZ)), dma((3, NZ)), dma, dma, dma, dma, dma((NZ,)), dma((NZ,)), dma((NY,)), dma((NY,)), dma, dma,
        ],
        compiler_params=pltpu.CompilerParams(
            collective_id=1, has_side_effects=True, vmem_limit_bytes=60 * 1024 * 1024
        ),
        name="gram",
    )(centered, stats)


def body(queries, keys, values, log_decay, gain):
    centered, stats = attend(queries, keys, values, log_decay, gain)
    shift, covariance = gram(centered, stats)
    return (shift.reshape(-1), covariance)


def solution(mesh):
    placed = (P("ctx", "head"), P("ctx", "head"), P("ctx", "head"), P("head", "ctx"), P("head"))
    return jax.shard_map(
        body,
        mesh=mesh,
        in_specs=placed,
        out_specs=(P("head"), P(("head", "ctx"), None)),
        check_vma=False,
    )
```

time: 514 us -> 108 us (0.21); the launches traced: 506 us -> 108 us
  blocking collectives: 267 us -> 0 us
  Pallas kernels: 0 us -> 105 us
  other arithmetic: 98.1 us -> 0 us
  waiting for transfers between devices: 49 us -> 0 us
  local copies, waits for them, and re-layouts: 38.8 us -> 2.84 us
  matrix products: 33.5 us -> 0 us
  between operations: 14.9 us -> 0.65 us
    all_gather x3 -> x0, blocking collectives: 135 us -> none  [the longest x2 86.3 us: merged(): pieces = jax.tree.map(lambda part: lax.all_gather(part, axis), value)]
    unnamed x1 -> x0, blocking collectives: 132 us -> none
    pallas_call x0 -> x2, Pallas kernels: none -> 105 us  [the longest x1 63.8 us: gram(): pl.pallas_call(gram_kernel, out_shape=(jax.ShapeDtypeStruct((8, D), F32),...]
    select_n x65 -> x0, other arithmetic: 76.6 us -> none  [the longest x63 73.9 us: turn(): jnp.where(position < mine, new, old)]
    ppermute x1 -> x0, waiting for transfers between devices: 41.7 us -> none  [from_partner(): return lax.ppermute(value, axis, pairs)]
    dot_general x15 -> x0, matrix products: 33.5 us -> none  [the longest x4 8.1 us: block_step(): jnp.einsum('hts,shd->thd', weights, value, preferred_element_type=jnp.flo...]
    dynamic_slice x71 -> x0, local copies, waits for them, and re-layouts: 12.1 us -> none  [the longest x8 9.43 us: run_blocks(): ending, raw = lax.scan(block_step, start, shaped)]
    reduce_sum x4 -> x0, other arithmetic: 8.75 us -> none  [the longest x1 4.16 us: body(): own_means = jnp.mean(attended.astype(jnp.float32), axis=0)]
  transfers between devices with their start and end apart: 3 -> 0, of which waited for: 3 -> 0; matrix products, arithmetic and copies ran while one was open for 4% -> 0% of each run, Pallas kernels for 0% -> 0%
where the time goes in v1:
time: 108 us
  Pallas kernels  105 us (97%)
  local copies, waits for them, and re-layouts  2.84 us (3%)
    pallas_call x1, Pallas kernels, gram(): pl.pallas_call(gram_kernel, out_shape=(jax.ShapeDtypeStruct((8, D), F32),...  63.8 us
    pallas_call x1, Pallas kernels, attend(): pl.pallas_call(attend_kernel, out_shape=(jax.ShapeDtypeStruct((count, wid...  40.8 us
    unnamed x2, local copies, waits for them, and re-layouts  2.84 us

profile of v1, /device:TPU:1, one launch (start us, length us, event | category | flops | bytes accessed | tf_op | source)
XLA Modules:
  0.0 108.1 jit_solution(9674886325506153617)
XLA Ops:
  0.6 40.8 %attend.1 = (bf16[1024,1024]{1,0:T(8,128)(2,1)}, f32[24,128]{1,0:T(8,128)}) custom-call(bf16[1024,1024]{1,0:T(8,128)(2,1)} %q_ref.1, bf16[1024,1024]{1,0:T(8,128)(2,1)} %k_ref.1, bf16[1024,1024]{1,0:T(8,128)(2,1)} %v_ref.1, f32[8,1024]{1,0:T(8,128)} %ld_ref.1, f32[8,128]{1,0:T(8,128)} %bitcast.3), custom_call_target="tpu_custom_call" | custom-call | tf_op jit(solution)/shard_map/attend/pallas_call | solution.py:261
  41.4 63.8 %gram.1 = (f32[8,128]{1,0:T(8,128)}, f32[16,2048]{1,0:T(8,128)}) custom-call(bf16[1024,1024]{1,0:T(8,128)(2,1)} %get-tuple-element.6.c_ref, f32[24,128]{1,0:T(8,128)} %get-tuple-element.7.st_ref), custom_call_target="tpu_custom_call" | custom-call | tf_op jit(solution)/shard_map/gram/pallas_call | solution.py:478
  105.2 1.3 %copy.9 = f32[1024]{0:T(1024)} copy(f32[1024]{0:T(1024)} %bitcast.2) | data formatting | bytes 8192
  106.5 1.6 %copy.10 = f32[16,2048]{1,0:T(8,128)} copy(f32[16,2048]{1,0:T(8,128)} %get-tuple-element.13) | data formatting | bytes 262144

commit v2 on v1

--- a/solution.py
+++ b/solution.py
@@ -290,11 +290,16 @@
     )(q, k, v, log_decay, gain.reshape(8, D))
 
 
+WIDE = 512
+SEGS = 6
+
+
 def gram_kernel(
     c_ref, st_ref, shift_ref, cov_ref,
-    theirs, full, grams, mates, sums, ylow, yhigh, ylast, yfirst, ynext, yprev, zsend, zin, strip, hop,
-    st1, stsum, stz, sty, off, offin,
-    s_x, r_x, s_c, r_c, s_y1, r_y1, s_y2, r_y2, s_z, r_z, s_h, r_h, s_s1, r_s1, s_sz, r_sz, s_sy, r_sy, s_o, r_o,
+    theirs, grams, mates, sums, ylow, yhigh, yfirst, ylast, ynext, yprev, zsend, zin, strip, hop,
+    means, ar, armate, stz, sty, left, right,
+    s_m, r_m, s_x, r_x, s_c, r_c, s_y1, r_y1, s_y2, r_y2, s_z, r_z, s_h, r_h,
+    s_s1, r_s1, s_sz, r_sz, s_sy, r_sy, s_g, r_g,
 ):
     y, z, core = place()
     parity = lax.rem(lax.axis_index("head"), 2)
@@ -312,27 +317,160 @@
 
     other_half = pl.ds(pl.multiple_of((1 - parity) * 512, 512), 512)
     half = pl.ds(pl.multiple_of(parity * 512, 512), 512)
-    swap = keep(send(c_ref.at[other_half], theirs, s_x, r_x, pair))
-    first = keep(send(st_ref, st1, s_s1, r_s1, mate))
-
-    def diagonal(i):
-        full[pl.ds(i * 256, 256), :] = lax.dot_general(
-            c_ref[:, i * 256 : i * 256 + 256], c_ref[...], TOK, preferred_element_type=F32
+    swap_mean = keep(send(st_ref.at[pl.ds(0, 8)], means.at[y, core, pl.ds(8, 8)], s_m, r_m, pair))
+    swaps = [
+        keep(
+            send(c_ref.at[other_half, pl.ds(k * WIDE, WIDE)], theirs.at[k], s_x.at[k], r_x.at[k], pair)
         )
+        for k in range(2)
+    ]
+    means[y, core, :8, :] = st_ref[:8, :]
+
+    def store(seg, first, value):
+        count = value.shape[0] // 32
+        grams[seg, pl.ds(first // 32, count)] = value.astype(BF16).reshape(count, 2, 16, WIDE)
+
+    def to_mate(seg):
+        return keep(send(grams.at[seg, :, 1 - core], mates.at[seg], s_c.at[seg], r_c.at[seg], mate))
+
+    def start_diag(k):
+        for i in range(4):
+            store(
+                k,
+                i * 256,
+                lax.dot_general(
+                    c_ref[:, i * 256 : i * 256 + 256],
+                    c_ref[:, k * WIDE : k * WIDE + WIDE],
+                    TOK,
+                    preferred_element_type=F32,
+                ),
+            )
+        return to_mate(k)
+
+    def start_cross(k):
+        for i in range(4):
+            store(
+                2 + k,
+                i * 256,
+                lax.dot_general(
+                    c_ref[half, i * 256 : i * 256 + 256], theirs[k], TOK, preferred_element_type=F32
+                ),
+            )
+        return to_mate(2 + k)
+
+    def start_turned(k):
+        for i in range(4):
+            store(
+                4 + k,
+                i * 256,
+                lax.dot_general(
+                    theirs[i // 2, :, (i % 2) * 256 : (i % 2) * 256 + 256],
+                    c_ref[half, k * WIDE : k * WIDE + WIDE],
+                    TOK,
+                    preferred_element_type=F32,
+                ),
+            )
+        return to_mate(4 + k)
 
     def merge(a, b):
         return jnp.concatenate(
-            [a[:8] + b[:8], jnp.maximum(a[8:16], b[8:16]), jnp.minimum(a[16:], b[16:])], axis=0
+            [a[:16] + b[:16], jnp.maximum(a[16:24], b[16:24]), jnp.minimum(a[24:], b[24:])], axis=0
         )
 
-    diagonal(0)
+    def add_mate(seg, copy):
+        copy.wait_recv()
+
+        def turn(i, carry):
+            four = pl.ds(i * 4, 4)
+            got = grams[seg, four, core].astype(F32) + mates[seg, four].astype(F32)
+            sums[seg, four] = got.astype(BF16)
+            return carry
+
+        lax.fori_loop(0, NZ, turn, 0)
+        part = sums.at[seg, pl.ds(far * NZ, NZ)]
+        edge = WIDE // 2
+        up = keep(
+            send(part.at[:, :, pl.ds(0, edge)], ylow.at[seg], s_y1.at[seg, 0], r_y1.at[seg, 0], at(north, z, core))
+        )
+        down = keep(
+            send(part.at[:, :, pl.ds(edge, edge)], yhigh.at[seg], s_y1.at[seg, 1], r_y1.at[seg, 1], at(south, z, core))
+        )
+        return up, down
+
+    def pass_on(seg, copies):
+        copies[0].wait_recv()
+        copies[1].wait_recv()
+        edge = WIDE // 2
+
+        def turn(i, carry):
+            two = pl.ds(i * 2, 2)
+            a = sums[seg, pl.ds(north * NZ + i * 2, 2)]
+            b = sums[seg, pl.ds(south * NZ + i * 2, 2)]
+            low = a[:, :, :edge].astype(F32) + ylow[seg, two].astype(F32)
+            high = b[:, :, edge:].astype(F32) + yhigh[seg, two].astype(F32)
+            ynext[seg, two, :, :edge] = low.astype(BF16)
+            ynext[seg, two, :, edge:] = a[:, :, edge:]
+            yprev[seg, two, :, :edge] = b[:, :, :edge]
+            yprev[seg, two, :, edge:] = high.astype(BF16)
+            return carry
+
+        lax.fori_loop(0, 4, turn, 0)
+        up = keep(send(ynext.at[seg], yfirst.at[seg], s_y2.at[seg, 0], r_y2.at[seg, 0], at(north, z, core)))
+        down = keep(send(yprev.at[seg], ylast.at[seg], s_y2.at[seg, 1], r_y2.at[seg, 1], at(south, z, core)))
+        return up, down
+
+    def to_z(seg, copies):
+        copies[0].wait_recv()
+        copies[1].wait_recv()
+        tall = 1024 if seg >= 4 else 0
+        wide = (1024 if seg in (2, 3) else 0) + (seg % 2) * WIDE
+        weight = 1024.0 if seg < 2 else 512.0
+        spread = weight * lax.dot_general(
+            left[:, pl.ds(pl.multiple_of(tall + y * 256, 256), 256)],
+            right[:, wide : wide + WIDE],
+            TOK,
+            preferred_element_type=F32,
+        )
+        spread = spread.reshape(NZ, 2, 16, WIDE)
+        spread = jnp.where(core == 0, spread[:, 0], spread[:, 1])
+        got = sums[seg, pl.ds(y * NZ, NZ)].astype(F32) + yfirst[seg].astype(F32)
+        got = got + ylast[seg].astype(F32) + spread
+        zsend[seg] = got.astype(BF16)
+        for i in range(1, NZ):
+            to = lax.rem(z + i, NZ)
+            keep(
+                send(zsend.at[seg, to], zin.at[seg, z], s_z.at[seg, i], r_z.at[seg, z], at(y, to, core))
+            )
+        zin[seg, z] = zsend[seg, z]
+
+    def from_z(seg):
+        for i in range(1, NZ):
+            frm = lax.rem(z + i, NZ)
+            arrived(
+                zsend.at[seg, frm], zin.at[seg, frm], s_z.at[seg, i], r_z.at[seg, frm], at(y, frm, core)
+            )
+        got = zin[seg, 0].astype(F32)
+        for j in range(1, NZ):
+            got = got + zin[seg, j].astype(F32)
+        return got
+
+    c0 = start_diag(0)
+    swap_mean.wait_recv()
+    ar[:16, :] = means[y, core]
+    ar[16:, :] = st_ref[8:, :]
+    first = keep(send(ar, armate, s_s1, r_s1, mate))
+    c1 = start_diag(1)
     first.wait_recv()
-    stz[z] = merge(st_ref[...], st1[...])
+    means[y, 1 - core] = armate[:16, :]
+    stz[z] = merge(ar[...], armate[...])
     for i in range(1, NZ):
         to = lax.rem(z + i, NZ)
         keep(send(stz.at[z], stz.at[z], s_sz.at[i], r_sz.at[z], at(y, to, core)))
-    diagonal(1)
-    diagonal(2)
+    for i in range(1, NY):
+        to = lax.rem(y + i, NY)
+        keep(send(means.at[y], means.at[y], s_g.at[i], r_g.at[y], at(to, z, core)))
+    p0 = add_mate(0, c0)
+    p1 = add_mate(1, c1)
     for i in range(1, NZ):
         frm = lax.rem(z + i, NZ)
         arrived(stz.at[frm], stz.at[frm], s_sz.at[i], r_sz.at[frm], at(y, frm, core))
@@ -340,132 +478,56 @@
     for i in range(1, NY):
         to = lax.rem(y + i, NY)
         keep(send(sty.at[y], sty.at[y], s_sy.at[i], r_sy.at[y], at(to, z, core)))
-    diagonal(3)
+    q0 = pass_on(0, p0)
+    q1 = pass_on(1, p1)
     for i in range(1, NY):
         frm = lax.rem(y + i, NY)
+        arrived(means.at[frm], means.at[frm], s_g.at[i], r_g.at[frm], at(frm, z, core))
         arrived(sty.at[frm], sty.at[frm], s_sy.at[i], r_sy.at[frm], at(frm, z, core))
     every = functools.reduce(merge, [sty[j] for j in range(NY)])
-    shift_ref[...] = (every[8:16] + every[16:]) / 2.0
-    off[...] = st_ref[:8, :] - every[:8] / 64.0
-    offset = keep(send(off, offin, s_o, r_o, pair))
-
-    def spread(tall, wide, weight, i):
-        column = jnp.transpose(tall)
-        rows = [
-            jnp.concatenate(
-                [
-                    weight * jnp.broadcast_to(column[:, h : h + 1], (D, D)) * wide[j : j + 1, :]
-                    for j in range(8)
-                ],
-                axis=1,
-            )
-            for h in (2 * i, 2 * i + 1)
-        ]
-        return jnp.concatenate(rows, axis=0)
-
-    def store(seg, i, value):
-        grams[seg, pl.ds(8 * i, 8)] = value.astype(BF16).reshape(8, 2, 16, 1024)
-
-    mine = off[...]
-    for i in range(4):
-        store(0, i, full[pl.ds(i * 256, 256), :] + spread(mine, mine, 1024.0, i))
-
-    def to_mate(seg):
-        return keep(send(grams.at[seg, :, 1 - core], mates.at[seg], s_c.at[seg], r_c.at[seg], mate))
-
-    def add_mate(seg, copy):
-        copy.wait_recv()
-
-        def turn(i, carry):
-            got = grams[seg, i, core].astype(F32) + mates[seg, i].astype(F32)
-            sums[seg, i // NZ, lax.rem(i, NZ)] = got.astype(BF16)
-            return carry
-
-        lax.fori_loop(0, NZ * NY, turn, 0)
-        up = keep(
-            send(sums.at[seg, far, :, :, pl.ds(0, 512)], ylow.at[seg], s_y1.at[seg, 0], r_y1.at[seg, 0], at(north, z, core))
-        )
-        down = keep(
-            send(sums.at[seg, far, :, :, pl.ds(512, 512)], yhigh.at[seg], s_y1.at[seg, 1], r_y1.at[seg, 1], at(south, z, core))
-        )
-        return up, down
-
-    def pass_on(seg, copies):
-        copies[0].wait_recv()
-        copies[1].wait_recv()
-
-        def turn(i, carry):
-            a, b = sums[seg, north, i].astype(F32), sums[seg, south, i].astype(F32)
-            low, high = ylow[seg, i].astype(F32), yhigh[seg, i].astype(F32)
-            ynext[seg, i] = jnp.concatenate([a[:, :512] + low, a[:, 512:]], axis=1).astype(BF16)
-            yprev[seg, i] = jnp.concatenate([b[:, :512], b[:, 512:] + high], axis=1).astype(BF16)
-            return carry
-
-        lax.fori_loop(0, NZ, turn, 0)
-        up = keep(send(ynext.at[seg], yfirst.at[seg], s_y2.at[seg, 0], r_y2.at[seg, 0], at(north, z, core)))
-        down = keep(send(yprev.at[seg], ylast.at[seg], s_y2.at[seg, 1], r_y2.at[seg, 1], at(south, z, core)))
-        return up, down
-
-    def to_z(seg, copies):
-        copies[0].wait_recv()
-        copies[1].wait_recv()
-
-        def turn(i, carry):
-            got = sums[seg, y, i].astype(F32) + yfirst[seg, i].astype(F32) + ylast[seg, i].astype(F32)
-            zsend[seg, i] = got.astype(BF16)
-            return carry
-
-        lax.fori_loop(0, NZ, turn, 0)
-        for i in range(1, NZ):
-            to = lax.rem(z + i, NZ)
-            keep(
-                send(zsend.at[seg, to], zin.at[seg, z], s_z.at[seg, i], r_z.at[seg, z], at(y, to, core))
-            )
-        zin[seg, z] = zsend[seg, z]
-
-    def from_z(seg):
-        for i in range(1, NZ):
-            frm = lax.rem(z + i, NZ)
-            arrived(
-                zsend.at[seg, frm], zin.at[seg, frm], s_z.at[seg, i], r_z.at[seg, frm], at(y, frm, core)
-            )
-        got = zin[seg, 0].astype(F32)
-        for j in range(1, NZ):
-            got = got + zin[seg, j].astype(F32)
-        return got
-
-    core0 = to_mate(0)
-    ph1 = add_mate(0, core0)
-    ph2 = pass_on(0, ph1)
-    offset.wait_recv()
-    swap.wait_recv()
-    pairs = offin[...]
-    for i in range(4):
-        value = lax.dot_general(
-            theirs[:, i * 256 : i * 256 + 256], c_ref[half, :], TOK, preferred_element_type=F32
-        )
-        store(1, i, value + spread(pairs, mine, 512.0, i))
-    core1 = to_mate(1)
-    for i in range(4):
-        value = lax.dot_general(
-            c_ref[half, i * 256 : i * 256 + 256], theirs[...], TOK, preferred_element_type=F32
-        )
-        store(2, i, value + spread(mine, pairs, 512.0, i))
-    core2 = to_mate(2)
-    to_z(0, ph2)
-    ph1a = add_mate(1, core1)
-    ph1b = add_mate(2, core2)
-    ph2a = pass_on(1, ph1a)
-    diag = from_z(0)
-    ph2b = pass_on(2, ph1b)
-    to_z(1, ph2a)
-    to_z(2, ph2b)
-    strip[...] = from_z(1)
-    final = keep(send(strip, hop, s_h, r_h, pair))
-    cross = from_z(2)
-    final.wait_recv()
-    cross = (cross + hop[...]) / 65536.0
-    diag = diag / 65536.0
+    shift_ref[...] = (every[16:24] + every[24:]) / 2.0
+    mu = every[:16] / 64.0
+    off = means[...].reshape(NY * 2, 16, D) - mu[None]
+    for j in range(16):
+        piece = off[:, j, :]
+        high = piece.astype(BF16)
+        low = (piece - high.astype(F32)).astype(BF16)
+        none = jnp.zeros_like(high)
+        cols = slice(j * D, j * D + D)
+        left[:, cols] = jnp.concatenate([high, high, low, none], axis=0)
+        right[:, cols] = jnp.concatenate([high, low, high, none], axis=0)
+    swaps[0].wait_recv()
+    c2 = start_cross(0)
+    to_z(0, q0)
+    p2 = add_mate(2, c2)
+    to_z(1, q1)
+    q2 = pass_on(2, p2)
+    swaps[1].wait_recv()
+    c4 = start_turned(0)
+    c5 = start_turned(1)
+    p4 = add_mate(4, c4)
+    c3 = start_cross(1)
+    p5 = add_mate(5, c5)
+    to_z(2, q2)
+    q4 = pass_on(4, p4)
+    p3 = add_mate(3, c3)
+    diag0 = from_z(0)
+    diag1 = from_z(1)
+    diag = jnp.concatenate([diag0, diag1], axis=1) / 65536.0
+    q5 = pass_on(5, p5)
+    to_z(4, q4)
+    q3 = pass_on(3, p3)
+    cross0 = from_z(2)
+    to_z(5, q5)
+    strip[0] = from_z(4)
+    hop0 = keep(send(strip.at[0], hop.at[0], s_h.at[0], r_h.at[0], pair))
+    to_z(3, q3)
+    strip[1] = from_z(5)
+    hop1 = keep(send(strip.at[1], hop.at[1], s_h.at[1], r_h.at[1], pair))
+    cross1 = from_z(3)
+    hop0.wait_recv()
+    hop1.wait_recv()
+    cross = jnp.concatenate([cross0 + hop[0], cross1 + hop[1]], axis=1) / 65536.0
     cov_ref[:, :1024] = jnp.where(parity == 0, diag, cross)
     cov_ref[:, 1024:] = jnp.where(parity == 0, cross, diag)
     for copy in out:
@@ -475,6 +537,8 @@
 def gram(centered, stats):
     vm = pl.BlockSpec(memory_space=pltpu.VMEM)
     dma = pltpu.SemaphoreType.DMA
+    block = pltpu.VMEM((SEGS, NZ, 16, WIDE), BF16)
+    edge = pltpu.VMEM((SEGS, NZ, 16, WIDE // 2), BF16)
     return pl.pallas_call(
         gram_kernel,
         out_shape=(
@@ -484,29 +548,24 @@
         in_specs=[vm] * 2,
         out_specs=(vm, vm),
         scratch_shapes=[
-            pltpu.VMEM((512, 1024), BF16),
-            pltpu.VMEM((1024, 1024), F32),
-            pltpu.VMEM((3, 32, 2, 16, 1024), BF16),
-            pltpu.VMEM((3, 32, 16, 1024), BF16),
-            pltpu.VMEM((3, NY, NZ, 16, 1024), BF16),
-            pltpu.VMEM((3, NZ, 16, 512), BF16),
-            pltpu.VMEM((3, NZ, 16, 512), BF16),
-            pltpu.VMEM((3, NZ, 16, 1024), BF16),
-            pltpu.VMEM((3, NZ, 16, 1024), BF16),
-            pltpu.VMEM((3, NZ, 16, 1024), BF16),
-            pltpu.VMEM((3, NZ, 16, 1024), BF16),
-            pltpu.VMEM((3, NZ, 16, 1024), BF16),
-            pltpu.VMEM((3, NZ, 16, 1024), BF16),
-            pltpu.VMEM((16, 1024), F32),
-            pltpu.VMEM((16, 1024), F32),
-            pltpu.VMEM((24, D), F32),
-            pltpu.VMEM((24, D), F32),
-            pltpu.VMEM((NZ, 24, D), F32),
-            pltpu.VMEM((NY, 24, D), F32),
-            pltpu.VMEM((8, D), F32),
-            pltpu.VMEM((8, D), F32),
-            dma, dma, dma((3,)), dma((3,)), dma((3, 2)), dma((3, 2)), dma((3, 2)), dma((3, 2)),
-            dma((3, NZ)), dma((3, NZ)), dma, dma, dma, dma, dma((NZ,)), dma((NZ,)), dma((NY,)), dma((NY,)), dma, dma,
+            pltpu.VMEM((2, 512, WIDE), BF16),
+            pltpu.VMEM((SEGS, 32, 2, 16, WIDE), BF16),
+            pltpu.VMEM((SEGS, 32, 16, WIDE), BF16),
+            pltpu.VMEM((SEGS, 32, 16, WIDE), BF16),
+            edge, edge, block, block, block, block, block, block,
+            pltpu.VMEM((2, 16, WIDE), F32),
+            pltpu.VMEM((2, 16, WIDE), F32),
+            pltpu.VMEM((NY, 2, 16, D), F32),
+            pltpu.VMEM((32, D), F32),
+            pltpu.VMEM((32, D), F32),
+            pltpu.VMEM((NZ, 32, D), F32),
+            pltpu.VMEM((NY, 32, D), F32),
+            pltpu.VMEM((32, 2048), BF16),
+            pltpu.VMEM((32, 2048), BF16),
+            dma, dma, dma((2,)), dma((2,)), dma((SEGS,)), dma((SEGS,)),
+            dma((SEGS, 2)), dma((SEGS, 2)), dma((SEGS, 2)), dma((SEGS, 2)),
+            dma((SEGS, NZ)), dma((SEGS, NZ)), dma((2,)), dma((2,)),
+            dma, dma, dma((NZ,)), dma((NZ,)), dma((NY,)), dma((NY,)), dma((NY,)), dma((NY,)),
         ],
         compiler_params=pltpu.CompilerParams(
             collective_id=1, has_side_effects=True, vmem_limit_bytes=60 * 1024 * 1024
@@ -515,9 +574,28 @@
     )(centered, stats)
 
 
+def hand_kernel(a_ref, b_ref, c_ref, d_ref):
+    c_ref[...] = a_ref[...]
+    d_ref[...] = b_ref[...]
+
+
+def hand_out(shift, covariance):
+    vm = pl.BlockSpec(memory_space=pltpu.VMEM)
+    return pl.pallas_call(
+        hand_kernel,
+        out_shape=(
+            jax.ShapeDtypeStruct(shift.shape, F32),
+            jax.ShapeDtypeStruct(covariance.shape, F32),
+        ),
+        in_specs=[vm] * 2,
+        out_specs=(vm, vm),
+        name="hand_out",
+    )(shift, covariance)
+
+
 def body(queries, keys, values, log_decay, gain):
     centered, stats = attend(queries, keys, values, log_decay, gain)
-    shift, covariance = gram(centered, stats)
+    shift, covariance = hand_out(*gram(centered, stats))
     return (shift.reshape(-1), covariance)
 
 

time: 108 us -> 101 us (0.935)
  Pallas kernels: 105 us -> 99.9 us
  local copies, waits for them, and re-layouts: 2.84 us -> 0 us
    pallas_call x1, Pallas kernels: 63.8 us -> 57.6 us  [gram(): pl.pallas_call(gram_kernel, out_shape=(jax.ShapeDtypeStruct((8, D), F32),...]
    unnamed x2 -> x0, local copies, waits for them, and re-layouts: 2.84 us -> none
    pallas_call x0 -> x1, Pallas kernels: none -> 1.58 us  [hand_out(): pl.pallas_call(hand_kernel, out_shape=(jax.ShapeDtypeStruct(shift.shape,...]
where the time goes in v2:
time: 101 us
  Pallas kernels  99.9 us (99%)
    pallas_call x1, Pallas kernels, gram(): pl.pallas_call(gram_kernel, out_shape=(jax.ShapeDtypeStruct((8, D), F32),...  57.6 us
    pallas_call x1, Pallas kernels, attend(): pl.pallas_call(attend_kernel, out_shape=(jax.ShapeDtypeStruct((count, wid...  40.8 us

profile of v2, /device:TPU:1, one launch (start us, length us, event | category | flops | bytes accessed | tf_op | source)
XLA Modules:
  0.0 100.6 jit_solution(9372249611185284114)
XLA Ops:
  0.6 40.8 %attend.1 = (bf16[1024,1024]{1,0:T(8,128)(2,1)}, f32[24,128]{1,0:T(8,128)}) custom-call(bf16[1024,1024]{1,0:T(8,128)(2,1)} %q_ref.1, bf16[1024,1024]{1,0:T(8,128)(2,1)} %k_ref.1, bf16[1024,1024]{1,0:T(8,128)(2,1)} %v_ref.1, f32[8,1024]{1,0:T(8,128)} %ld_ref.1, f32[8,128]{1,0:T(8,128)} %bitcast.2), custom_call_target="tpu_custom_call" | custom-call | tf_op jit(solution)/shard_map/attend/pallas_call | solution.py:261
  41.4 57.6 %gram.1 = (f32[8,128]{1,0:T(8,128)}, f32[16,2048]{1,0:T(8,128)}) custom-call(bf16[1024,1024]{1,0:T(8,128)(2,1)} %get-tuple-element.8.c_ref, f32[24,128]{1,0:T(8,128)} %get-tuple-element.9.st_ref), custom_call_target="tpu_custom_call" | custom-call | tf_op jit(solution)/shard_map/gram/pallas_call | solution.py:542
  99.0 1.6 %hand_out.1 = (f32[8,128]{1,0:T(8,128)}, f32[16,2048]{1,0:T(8,128)}) custom-call(f32[8,128]{1,0:T(8,128)} %get-tuple-element.10.a_ref, f32[16,2048]{1,0:T(8,128)} %get-tuple-element.11.b_ref), custom_call_target="tpu_custom_call" | custom-call | tf_op jit(solution)/shard_map/hand_out/pallas_call | solution.py:584

commit v3 on v0

v3 whole, which is shorter than its diff:
```python
import functools

import jax
import jax.numpy as jnp
from jax import lax
from jax.experimental import pallas as pl
from jax.experimental.pallas import tpu as pltpu
from jax.sharding import PartitionSpec as P

D = 128
SPAN = 256
NZ = 8
NY = 4
F32 = jnp.float32
BF16 = jnp.bfloat16
MESH = pl.DeviceIdType.MESH
TOK = (((0,), (0,)), ((), ()))
LAST = (((1,), (1,)), ((), ()))


def place():
    me = lax.axis_index("ctx")
    core = lax.rem(me, 2)
    z = lax.rem(me // 2, NZ)
    y = me // (2 * NZ)
    return y, z, core


def at(y, z, core):
    return {"ctx": (y * NZ + z) * 2 + core}


def greet(peers):
    barrier = pltpu.get_barrier_semaphore()
    for peer in peers:
        pl.semaphore_signal(barrier, inc=1, device_id=peer, device_id_type=MESH)
    return lambda: pl.semaphore_wait(barrier, len(peers))


def send(src, dst, ssem, rsem, peer):
    copy = pltpu.make_async_remote_copy(
        src_ref=src, dst_ref=dst, send_sem=ssem, recv_sem=rsem, device_id=peer, device_id_type=MESH
    )
    copy.start()
    return copy


def arrived(src, dst, ssem, rsem, peer):
    pltpu.make_async_remote_copy(
        src_ref=src, dst_ref=dst, send_sem=ssem, recv_sem=rsem, device_id=peer, device_id_type=MESH
    ).wait_recv()


def plane_peers(y, z, core):
    peers = [at(y, z, 1 - core)]
    peers += [at(y, lax.rem(z + i, NZ), core) for i in range(1, NZ)]
    peers += [at(lax.rem(y + i, NY), z, core) for i in range(1, NY)]
    return peers


PIECE = 32
DIAG, CROSS, TURNED = 0, 1, 2
SEGMENTS = (
    (DIAG, 0, 512),
    (DIAG, 512, 512),
    (CROSS, 0, 512),
    (CROSS, 512, 256),
    (TURNED, 0, 512),
    (TURNED, 512, 512),
    (CROSS, 768, 256),
)
SEGS = len(SEGMENTS)


def expand(piece):
    return jnp.concatenate(
        [jnp.broadcast_to(piece[PIECE + i : PIECE + i + 1], (16, D)) for i in range(2)], axis=0
    )


def join(first, second):
    return expand(second) * first[:PIECE] + second[:PIECE], first[PIECE:] * second[PIECE:]


def kernel(
    q_hbm, k_hbm, v_hbm, ld_ref, gain_ref, shift_ref, cov_ref,
    q_ref, k_ref, v_ref, c_ref, st_ref,
    cum, col, inner, upd, part, other, chip, zin, pre, yin, back, chipin, give, sin,
    theirs, strip, hop, means, armate, stz, sty, off, offin, left, right,
    grams, mates, sums, ylow, yhigh, yfirst, ylast, ynext, yprev, zsend, zgot,
    s_in, s_core, r_core, s_z, r_z, s_y, r_y, s_zb, r_zb, s_cb, r_cb,
    s_m, r_m, s_x, r_x, s_c, r_c, s_y1, r_y1, s_y2, r_y2, s_zz, r_zz, s_h, r_h,
    s_s1, r_s1, s_sz, r_sz, s_sy, r_sy, s_g, r_g,
):
    y, z, core = place()
    parity = lax.rem(lax.axis_index("head"), 2)
    pair = {"head": lax.axis_index("head") + 1 - 2 * parity}
    mate = at(y, z, 1 - core)
    north, south = lax.rem(y + 1, NY), lax.rem(y + NY - 1, NY)
    far = lax.rem(y + 2, NY)
    ready = greet(plane_peers(y, z, core) + [pair])
    out = []

    def keep(copy):
        out.append(copy)
        return copy

    def load(src, dst, sem):
        copy = pltpu.make_async_copy(src, dst, sem)
        copy.start()
        return copy

    def half_of(ref, g):
        return ref.at[:, pl.ds(g * 512, 512)]

    kv_in = [
        (
            load(half_of(k_hbm, g), half_of(k_ref, g), s_in.at[2 * g]),
            load(half_of(v_hbm, g), half_of(v_ref, g), s_in.at[2 * g + 1]),
        )
        for g in range(2)
    ]
    q_in = load(q_hbm, q_ref, s_in.at[4])

    total = ld_ref[...]
    lane = lax.rem(lax.broadcasted_iota(jnp.int32, total.shape, 1), SPAN)
    step = 1
    while step < SPAN:
        total = total + jnp.where(lane >= step, pltpu.roll(total, step, 1), 0.0)
        step *= 2
    cum[...] = total
    turned = jnp.transpose(total)
    for head in range(8):
        col[head] = jnp.broadcast_to(turned[:, head : head + 1], (4 * SPAN, D))
    part[...] = jnp.zeros_like(part)

    def lanes(head):
        return pl.ds(pl.multiple_of(head * D, D), D)

    def both_heads(work):
        def turn(i, carry):
            work(i)
            return carry

        lax.fori_loop(0, 2, turn, 0)

    def update(g, owning):
        def one(i):
            head = 4 * g + 2 * owning + i
            ending = jnp.zeros((D, D), F32)
            decay = jnp.zeros((1, D), F32)
            for b in range(4):
                rows = pl.ds(b * SPAN, SPAN)
                last = col[head, pl.ds(b * SPAN + SPAN - 1, 1), :]
                scaled = v_ref[rows, lanes(head)].astype(F32) * jnp.exp(last - col[head, rows, :])
                high = scaled.astype(BF16)
                low = (scaled - high.astype(F32)).astype(BF16)
                both = lax.dot_general(
                    k_ref[rows, lanes(head)],
                    jnp.concatenate([high, low], axis=1),
                    TOK,
                    preferred_element_type=F32,
                )
                new = both[:, :D] + both[:, D:]
                upd[head, b] = new
                ending = jnp.exp(last) * ending + new
                decay = decay + last
            for owner in range(NZ):
                part[g, owning, owner, pl.ds(pl.multiple_of(i * 16, 16), 16), :] = ending[
                    owner * 16 : owner * 16 + 16
                ]
                part[g, owning, owner, pl.ds(PIECE + i, 1), :] = jnp.exp(decay)

        both_heads(one)

    later = lax.broadcasted_iota(jnp.int32, (SPAN, SPAN), 0) >= lax.broadcasted_iota(
        jnp.int32, (SPAN, SPAN), 1
    )

    def within(lo, hi):
        def turn(head, carry):
            for b in range(4):
                rows = pl.ds(b * SPAN, SPAN)
                scores = lax.dot_general(
                    q_ref[rows, lanes(head)],
                    k_ref[rows, lanes(head)],
                    LAST,
                    preferred_element_type=F32,
                )
                mine = col[head, rows, :]
                diff = jnp.concatenate([mine, mine], axis=1) - cum[pl.ds(head, 1), rows]
                weights = jnp.where(later, scores * jnp.exp(jnp.minimum(diff, 0.0)), 0.0)
                inner[head, rows, :] = jnp.dot(
                    weights.astype(BF16), v_ref[rows, lanes(head)], preferred_element_type=F32
                )
            return carry

        lax.fori_loop(lo, hi, turn, 0)

    def to_core(g):
        return keep(send(part.at[g, 1 - core], other.at[g], s_core.at[g], r_core.at[g], mate))

    def to_owners(g, copy):
        copy.wait_recv()

        def combine(owner, carry):
            mine, theirs_ = part[g, core, owner], other[g, owner]
            first = jnp.where(core == 0, mine, theirs_)
            second = jnp.where(core == 0, theirs_, mine)
            state, decay = join(first, second)
            chip[g, owner, :PIECE, :] = state
            chip[g, owner, PIECE:, :] = decay
            return carry

        lax.fori_loop(0, NZ, combine, 0)
        for i in range(1, NZ):
            to = lax.rem(z + i, NZ)
            keep(send(chip.at[g, to], zin.at[g, z], s_z.at[g, i], r_z.at[g, z], at(y, to, core)))
        zin[g, z] = chip[g, z]

    def to_rows(g):
        for i in range(1, NZ):
            frm = lax.rem(z + i, NZ)
            arrived(chip.at[g, frm], zin.at[g, frm], s_z.at[g, i], r_z.at[g, frm], at(y, frm, core))
        state, decay = jnp.zeros((PIECE, D), F32), jnp.ones((8, D), F32)
        for j in range(NZ):
            pre[g, j, :PIECE, :] = state
            pre[g, j, PIECE:, :] = decay
            state, decay = join(jnp.concatenate([state, decay], axis=0), zin[g, j])
        yin[g, y, :PIECE, :] = state
        yin[g, y, PIECE:, :] = decay
        for i in range(1, NY):
            to = lax.rem(y + i, NY)
            keep(send(yin.at[g, y], yin.at[g, y], s_y.at[g, i], r_y.at[g, y], at(to, z, core)))

    def to_chips(g):
        for i in range(1, NY):
            frm = lax.rem(y + i, NY)
            arrived(yin.at[g, frm], yin.at[g, frm], s_y.at[g, i], r_y.at[g, frm], at(frm, z, core))
        row = jnp.zeros((PIECE, D), F32)
        for j in range(NY):
            piece = yin[g, j]
            row = jnp.where(j < y, expand(piece) * row + piece[:PIECE], row)
        for j in range(NZ):
            piece = pre[g, j]
            back[g, j] = expand(piece) * row + piece[:PIECE]
        for i in range(1, NZ):
            to = lax.rem(z + i, NZ)
            keep(send(back.at[g, to], chipin.at[g, z], s_zb.at[g, i], r_zb.at[g, z], at(y, to, core)))
        chipin[g, z] = back[g, z]

    def to_cores(g):
        for i in range(1, NZ):
            frm = lax.rem(z + i, NZ)
            arrived(
                back.at[g, frm], chipin.at[g, frm], s_zb.at[g, i], r_zb.at[g, frm], at(y, frm, core)
            )

        def split(owner, carry):
            lead = jnp.where(core == 0, part[g, core, owner], other[g, owner])
            early = chipin[g, owner]
            late = expand(lead) * early + lead[:PIECE]
            give[g, owner] = jnp.where(core == 0, late, early)
            sin[g, core, owner] = jnp.where(core == 0, early, late)
            return carry

        lax.fori_loop(0, NZ, split, 0)
        return keep(send(give.at[g], sin.at[g, core], s_cb.at[g], r_cb.at[g], mate))

    def finish(g, owning):
        def one(i):
            head = 4 * g + 2 * owning + i
            state = jnp.concatenate(
                [
                    sin[g, owning, owner, pl.ds(pl.multiple_of(i * 16, 16), 16), :]
                    for owner in range(NZ)
                ],
                axis=0,
            )
            gain = gain_ref[pl.ds(head, 1), :]
            mean = jnp.zeros((1, D), F32)
            top = bottom = None
            for b in range(4):
                rows = pl.ds(b * SPAN, SPAN)
                high = state.astype(BF16)
                low = (state - high.astype(F32)).astype(BF16)
                both = jnp.dot(
                    q_ref[rows, lanes(head)],
                    jnp.concatenate([high, low], axis=1),
                    preferred_element_type=F32,
                )
                raw = inner[head, rows, :] + jnp.exp(col[head, rows, :]) * (both[:, :D] + both[:, D:])
                scale = jnp.sqrt(jnp.mean(raw * raw, axis=1, keepdims=True) + 1e-06)
                done = (raw / scale * gain).astype(BF16).astype(F32)
                mean = mean + jnp.sum(done, axis=0, keepdims=True)
                high_b = jnp.max(done, axis=0, keepdims=True)
                low_b = jnp.min(done, axis=0, keepdims=True)
                top = high_b if top is None else jnp.maximum(top, high_b)
                bottom = low_b if bottom is None else jnp.minimum(bottom, low_b)
                inner[head, rows, :] = done
                if b < 3:
                    last = col[head, pl.ds(b * SPAN + SPAN - 1, 1), :]
                    state = jnp.exp(last) * state + upd[head, b]
            mean = mean / (4 * SPAN)
            for b in range(4):
                rows = pl.ds(b * SPAN, SPAN)
                c_ref[rows, lanes(head)] = (inner[head, rows, :] - mean).astype(BF16)
            st_ref[pl.ds(head, 1), :] = mean
            st_ref[pl.ds(8 + head, 1), :] = top
            st_ref[pl.ds(16 + head, 1), :] = bottom

        both_heads(one)

    other_half = pl.ds(pl.multiple_of((1 - parity) * 512, 512), 512)
    half = pl.ds(pl.multiple_of(parity * 512, 512), 512)

    def columns(j):
        return pl.ds(pl.multiple_of(j * 256, 256), 256)

    def to_pair(j):
        return keep(
            send(
                c_ref.at[other_half, columns(j)],
                theirs.at[:, columns(j)],
                s_x.at[j],
                r_x.at[j],
                pair,
            )
        )

    def from_pair(j):
        arrived(
            c_ref.at[other_half, columns(j)], theirs.at[:, columns(j)], s_x.at[j], r_x.at[j], pair
        )

    def to_mate(seg):
        return keep(send(grams[seg].at[:, 1 - core], mates[seg], s_c.at[seg], r_c.at[seg], mate))

    def begin(seg):
        kind, first, wide = SEGMENTS[seg]
        cols = slice(first, first + wide)
        for i in range(4):
            rows = slice(i * 256, i * 256 + 256)
            if kind == DIAG:
                a, b = c_ref[:, rows], c_ref[:, cols]
            elif kind == CROSS:
                a, b = c_ref[half, rows], theirs[:, cols]
            else:
                a, b = theirs[:, rows], c_ref[half, cols]
            value = lax.dot_general(a, b, TOK, preferred_element_type=F32)
            grams[seg][pl.ds(8 * i, 8)] = value.astype(BF16).reshape(8, 2, 16, wide)
        return to_mate(seg)

    def merge(a, b):
        return jnp.concatenate(
            [a[:8] + b[:8], jnp.maximum(a[8:16], b[8:16]), jnp.minimum(a[16:], b[16:])], axis=0
        )

    def add_mate(seg, copy):
        copy.wait_recv()

        def turn(i, carry):
            four = pl.ds(i * 4, 4)
            got = grams[seg][four, core].astype(F32) + mates[seg][four].astype(F32)
            sums[seg][four] = got.astype(BF16)
            return carry

        lax.fori_loop(0, NZ, turn, 0)
        block = sums[seg].at[pl.ds(far * NZ, NZ)]
        edge = SEGMENTS[seg][2] // 2
        up = keep(
            send(block.at[:, :, pl.ds(0, edge)], ylow[seg], s_y1.at[seg, 0], r_y1.at[seg, 0], at(north, z, core))
        )
        down = keep(
            send(block.at[:, :, pl.ds(edge, edge)], yhigh[seg], s_y1.at[seg, 1], r_y1.at[seg, 1], at(south, z, core))
        )
        return up, down

    def pass_on(seg, copies):
        copies[0].wait_recv()
        copies[1].wait_recv()
        edge = SEGMENTS[seg][2] // 2

        def turn(i, carry):
            two = pl.ds(i * 2, 2)
            a = sums[seg][pl.ds(north * NZ + i * 2, 2)]
            b = sums[seg][pl.ds(south * NZ + i * 2, 2)]
            low = a[:, :, :edge].astype(F32) + ylow[seg][two].astype(F32)
            high = b[:, :, edge:].astype(F32) + yhigh[seg][two].astype(F32)
            ynext[seg][two, :, :edge] = low.astype(BF16)
            ynext[seg][two, :, edge:] = a[:, :, edge:]
            yprev[seg][two, :, :edge] = b[:, :, :edge]
            yprev[seg][two, :, edge:] = high.astype(BF16)
            return carry

        lax.fori_loop(0, 4, turn, 0)
        up = keep(send(ynext[seg], yfirst[seg], s_y2.at[seg, 0], r_y2.at[seg, 0], at(north, z, core)))
        down = keep(send(yprev[seg], ylast[seg], s_y2.at[seg, 1], r_y2.at[seg, 1], at(south, z, core)))
        return up, down

    def to_z(seg, copies):
        copies[0].wait_recv()
        copies[1].wait_recv()
        kind, first, wide = SEGMENTS[seg]
        tall = 1024 if kind == TURNED else 0
        start = first + (1024 if kind == CROSS else 0)
        spread = lax.dot_general(
            left[:, pl.ds(pl.multiple_of(tall + y * 256, 256), 256)],
            right[:, start : start + wide],
            TOK,
            preferred_element_type=F32,
        )
        spread = spread.reshape(NZ, 2, 16, wide) * (1024.0 if kind == DIAG else 512.0)
        spread = jnp.where(core == 0, spread[:, 0], spread[:, 1])
        got = sums[seg][pl.ds(y * NZ, NZ)].astype(F32) + yfirst[seg][...].astype(F32)
        got = got + ylast[seg][...].astype(F32) + spread
        zsend[seg][...] = got.astype(BF16)
        for i in range(1, NZ):
            to = lax.rem(z + i, NZ)
            keep(
                send(zsend[seg].at[to], zgot[seg].at[z], s_zz.at[seg, i], r_zz.at[seg, z], at(y, to, core))
            )
        zgot[seg][z] = zsend[seg][z]

    def from_z(seg):
        for i in range(1, NZ):
            frm = lax.rem(z + i, NZ)
            arrived(
                zsend[seg].at[frm], zgot[seg].at[frm], s_zz.at[seg, i], r_zz.at[seg, frm], at(y, frm, core)
            )
        got = zgot[seg][0].astype(F32)
        for j in range(1, NZ):
            got = got + zgot[seg][j].astype(F32)
        return got

    def kv_ready(g):
        kv_in[g][0].wait()
        kv_in[g][1].wait()

    kv_ready(0)
    update(0, 1 - core)
    ready()
    b0 = to_core(0)
    update(0, core)
    kv_ready(1)
    update(1, 1 - core)
    b1 = to_core(1)
    to_owners(0, b0)
    update(1, core)
    to_owners(1, b1)
    q_in.wait()
    within(0, 6)
    to_rows(0)
    within(6, 7)
    to_rows(1)
    within(7, 8)
    to_chips(0)
    to_chips(1)
    e0 = to_cores(0)
    finish(0, core)
    to_pair(core)
    e0.wait_recv()
    finish(0, 1 - core)
    to_pair(1 - core)
    e1 = to_cores(1)
    finish(1, core)
    e1.wait_recv()
    finish(1, 1 - core)
    first = keep(send(st_ref, armate, s_s1, r_s1, mate))
    to_pair(2)
    to_pair(3)
    means[y, core] = st_ref[:8, :]

    def spread_rows(source, base):
        for j in range(8):
            piece = source[:, j, :]
            high = piece.astype(BF16)
            low = (piece - high.astype(F32)).astype(BF16)
            none = jnp.zeros_like(high)
            cols = slice(base + j * D, base + j * D + D)
            left[:, cols] = jnp.concatenate([high, high, low, none], axis=0)
            right[:, cols] = jnp.concatenate([high, low, high, none], axis=0)

    c0 = begin(0)
    first.wait_recv()
    means[y, 1 - core] = armate[:8, :]
    stz[z] = merge(st_ref[...], armate[...])
    for i in range(1, NZ):
        to = lax.rem(z + i, NZ)
        keep(send(stz.at[z], stz.at[z], s_sz.at[i], r_sz.at[z], at(y, to, core)))
    for i in range(1, NY):
        to = lax.rem(y + i, NY)
        keep(send(means.at[y], means.at[y], s_g.at[i], r_g.at[y], at(to, z, core)))
    c1 = begin(1)
    p0 = add_mate(0, c0)
    p1 = add_mate(1, c1)
    q0 = pass_on(0, p0)
    from_pair(core)
    from_pair(1 - core)
    c2 = begin(2)
    q1 = pass_on(1, p1)
    for i in range(1, NZ):
        frm = lax.rem(z + i, NZ)
        arrived(stz.at[frm], stz.at[frm], s_sz.at[i], r_sz.at[frm], at(y, frm, core))
    sty[y] = functools.reduce(merge, [stz[j] for j in range(NZ)])
    for i in range(1, NY):
        to = lax.rem(y + i, NY)
        keep(send(sty.at[y], sty.at[y], s_sy.at[i], r_sy.at[y], at(to, z, core)))
    p2 = add_mate(2, c2)
    from_pair(2)
    c3 = begin(3)
    for i in range(1, NY):
        frm = lax.rem(y + i, NY)
        arrived(means.at[frm], means.at[frm], s_g.at[i], r_g.at[frm], at(frm, z, core))
        arrived(sty.at[frm], sty.at[frm], s_sy.at[i], r_sy.at[frm], at(frm, z, core))
    every = functools.reduce(merge, [sty[j] for j in range(NY)])
    shift_ref[...] = (every[8:16] + every[16:]) / 2.0
    off[...] = means[...].reshape(NY * 2, 8, D) - (every[:8] / 64.0)[None]
    offset = keep(send(off, offin, s_m, r_m, pair))
    spread_rows(off, 0)
    to_z(0, q0)
    to_z(1, q1)
    q2 = pass_on(2, p2)
    p3 = add_mate(3, c3)
    from_pair(3)
    c4 = begin(4)
    c5 = begin(5)
    p4 = add_mate(4, c4)
    c6 = begin(6)
    p5 = add_mate(5, c5)
    q3 = pass_on(3, p3)
    p6 = add_mate(6, c6)
    offset.wait_recv()
    spread_rows(offin, 1024)
    to_z(2, q2)
    q4 = pass_on(4, p4)
    to_z(3, q3)
    q5 = pass_on(5, p5)
    q6 = pass_on(6, p6)
    diag = jnp.concatenate([from_z(0), from_z(1)], axis=1) / 65536.0
    to_z(4, q4)
    to_z(5, q5)
    to_z(6, q6)
    cross0 = from_z(2)
    cross1 = from_z(3)
    strip[0] = from_z(4)
    hop0 = keep(send(strip.at[0], hop.at[0], s_h.at[0], r_h.at[0], pair))
    strip[1] = from_z(5)
    hop1 = keep(send(strip.at[1], hop.at[1], s_h.at[1], r_h.at[1], pair))
    cross2 = from_z(6)
    hop0.wait_recv()
    hop1.wait_recv()
    cross = jnp.concatenate([cross0, cross1, cross2], axis=1)
    cross = (cross + jnp.concatenate([hop[0], hop[1]], axis=1)) / 65536.0
    cov_ref[:, :1024] = jnp.where(parity == 0, diag, cross)
    cov_ref[:, 1024:] = jnp.where(parity == 0, cross, diag)
    for copy in out:
        copy.wait_send()


def whole(q, k, v, log_decay, gain):
    count, width = q.shape
    vm = pl.BlockSpec(memory_space=pltpu.VMEM)
    hbm = pl.BlockSpec(memory_space=pl.ANY)
    dma = pltpu.SemaphoreType.DMA

    def f32(*shape):
        return pltpu.VMEM(shape, F32)

    def bf16(*shape):
        return pltpu.VMEM(shape, BF16)

    def per_segment(*shape, share=1):
        return tuple(pltpu.VMEM((*shape, wide // share), BF16) for _, _, wide in SEGMENTS)

    return pl.pallas_call(
        kernel,
        out_shape=(
            jax.ShapeDtypeStruct((8, D), F32),
            jax.ShapeDtypeStruct((16, 2048), F32),
        ),
        in_specs=[hbm, hbm, hbm, vm, vm],
        out_specs=(vm, vm),
        scratch_shapes=[
            bf16(count, width),
            bf16(count, width),
            bf16(count, width),
            bf16(count, width),
            f32(24, D),
            f32(8, 1024),
            f32(8, 1024, D),
            f32(8, 1024, D),
            f32(8, 4, D, D),
            f32(2, 2, NZ, PIECE + 8, D),
            f32(2, NZ, PIECE + 8, D),
            f32(2, NZ, PIECE + 8, D),
            f32(2, NZ, PIECE + 8, D),
            f32(2, NZ, PIECE + 8, D),
            f32(2, NY, PIECE + 8, D),
            f32(2, NZ, PIECE, D),
            f32(2, NZ, PIECE, D),
            f32(2, NZ, PIECE, D),
            f32(2, 2, NZ, PIECE, D),
            bf16(512, 1024),
            f32(2, 16, 512),
            f32(2, 16, 512),
            f32(NY, 2, 8, D),
            f32(24, D),
            f32(NZ, 24, D),
            f32(NY, 24, D),
            f32(2 * NY, 8, D),
            f32(2 * NY, 8, D),
            bf16(32, 2048),
            bf16(32, 2048),
            per_segment(32, 2, 16),
            per_segment(32, 16),
            per_segment(32, 16),
            per_segment(NZ, 16, share=2),
            per_segment(NZ, 16, share=2),
            per_segment(NZ, 16),
            per_segment(NZ, 16),
            per_segment(NZ, 16),
            per_segment(NZ, 16),
            per_segment(NZ, 16),
            per_segment(NZ, 16),
            dma((5,)), dma((2,)), dma((2,)), dma((2, NZ)), dma((2, NZ)), dma((2, NY)), dma((2, NY)),
            dma((2, NZ)), dma((2, NZ)), dma((2,)), dma((2,)),
            dma, dma, dma((4,)), dma((4,)), dma((SEGS,)), dma((SEGS,)),
            dma((SEGS, 2)), dma((SEGS, 2)), dma((SEGS, 2)), dma((SEGS, 2)),
            dma((SEGS, NZ)), dma((SEGS, NZ)), dma((2,)), dma((2,)),
            dma, dma, dma((NZ,)), dma((NZ,)), dma((NY,)), dma((NY,)), dma((NY,)), dma((NY,)),
        ],
        compiler_params=pltpu.CompilerParams(
            collective_id=0, has_side_effects=True, vmem_limit_bytes=60 * 1024 * 1024
        ),
        name="whole",
    )(q, k, v, log_decay, gain.reshape(8, D))


def hand_kernel(a_ref, b_ref, c_ref, d_ref):
    c_ref[...] = a_ref[...]
    d_ref[...] = b_ref[...]


def hand_out(shift, covariance):
    vm = pl.BlockSpec(memory_space=pltpu.VMEM)
    return pl.pallas_call(
        hand_kernel,
        out_shape=(
            jax.ShapeDtypeStruct(shift.shape, F32),
            jax.ShapeDtypeStruct(covariance.shape, F32),
        ),
        in_specs=[vm] * 2,
        out_specs=(vm, vm),
        name="hand_out",
    )(shift, covariance)


def body(queries, keys, values, log_decay, gain):
    shift, covariance = hand_out(*whole(queries, keys, values, log_decay, gain))
    return (shift.reshape(-1), covariance)


def solution(mesh):
    placed = (P("ctx", "head"), P("ctx", "head"), P("ctx", "head"), P("head", "ctx"), P("head"))
    return jax.shard_map(
        body,
        mesh=mesh,
        in_specs=placed,
        out_specs=(P("head"), P(("head", "ctx"), None)),
        check_vma=False,
    )
```

time: 514 us -> 84.4 us (0.16); the launches traced: 506 us -> 84.2 us
  blocking collectives: 267 us -> 0 us
  other arithmetic: 98.1 us -> 0 us
  Pallas kernels: 0 us -> 83.6 us
  waiting for transfers between devices: 49 us -> 0 us
  local copies, waits for them, and re-layouts: 38.8 us -> 0 us
  matrix products: 33.5 us -> 0 us
  between operations: 14.9 us -> 0.64 us
    all_gather x3 -> x0, blocking collectives: 135 us -> none  [the longest x2 86.3 us: merged(): pieces = jax.tree.map(lambda part: lax.all_gather(part, axis), value)]
    unnamed x1 -> x0, blocking collectives: 132 us -> none
    pallas_call x0 -> x2, Pallas kernels: none -> 83.6 us  [the longest x1 82 us: whole(): pl.pallas_call(kernel, out_shape=(jax.ShapeDtypeStruct((8, D), F32), jax....]
    select_n x65 -> x0, other arithmetic: 76.6 us -> none  [the longest x63 73.9 us: turn(): jnp.where(position < mine, new, old)]
    ppermute x1 -> x0, waiting for transfers between devices: 41.7 us -> none  [from_partner(): return lax.ppermute(value, axis, pairs)]
    dot_general x15 -> x0, matrix products: 33.5 us -> none  [the longest x4 8.1 us: block_step(): jnp.einsum('hts,shd->thd', weights, value, preferred_element_type=jnp.flo...]
    dynamic_slice x71 -> x0, local copies, waits for them, and re-layouts: 12.1 us -> none  [the longest x8 9.43 us: run_blocks(): ending, raw = lax.scan(block_step, start, shaped)]
    unnamed x26 -> x0, local copies, waits for them, and re-layouts: 9.41 us -> none
  transfers between devices with their start and end apart: 3 -> 0, of which waited for: 3 -> 0; matrix products, arithmetic and copies ran while one was open for 4% -> 0% of each run, Pallas kernels for 0% -> 0%
where the time goes in v3:
time: 84.4 us; the launch traced here: 84.2 us
  Pallas kernels  83.6 us (99%)
    pallas_call x1, Pallas kernels, whole(): pl.pallas_call(kernel, out_shape=(jax.ShapeDtypeStruct((8, D), F32), jax....  82 us

profile of v3, /device:TPU:1, one launch (start us, length us, event | category | flops | bytes accessed | tf_op | source)
XLA Modules:
  0.0 84.2 jit_solution(18169803040387574945)
XLA Ops:
  0.6 82.0 %whole.1 = (f32[8,128]{1,0:T(8,128)}, f32[16,2048]{1,0:T(8,128)}) custom-call(bf16[1024,1024]{1,0:T(8,128)(2,1)} %q_hbm.1, bf16[1024,1024]{1,0:T(8,128)(2,1)} %k_hbm.1, bf16[1024,1024]{1,0:T(8,128)(2,1)} %v_hbm.1, f32[8,1024]{1,0:T(8,128)} %ld_ref.1, f32[8,128]{1,0:T(8,128)} %bitcast.2), custom_call_target="tpu_custom_call" | custom-call | tf_op jit(solution)/shard_map/whole/pallas_call | solution.py:576
  82.7 1.6 %hand_out.1 = (f32[8,128]{1,0:T(8,128)}, f32[16,2048]{1,0:T(8,128)}) custom-call(f32[8,128]{1,0:T(8,128)} %get-tuple-element.6.a_ref, f32[16,2048]{1,0:T(8,128)} %get-tuple-element.7.b_ref), custom_call_target="tpu_custom_call" | custom-call | tf_op jit(solution)/shard_map/hand_out/pallas_call | solution.py:647

commit v4 on v3

--- a/solution.py
+++ b/solution.py
@@ -83,13 +83,13 @@
 
 
 def kernel(
-    q_hbm, k_hbm, v_hbm, ld_ref, gain_ref, shift_ref, cov_ref,
+    q_hbm, k_hbm, v_hbm, ld_ref, gain_ref, shift_hbm, cov_hbm,
     q_ref, k_ref, v_ref, c_ref, st_ref,
     cum, col, inner, upd, part, other, chip, zin, pre, yin, back, chipin, give, sin,
-    theirs, strip, hop, means, armate, stz, sty, off, offin, left, right,
+    theirs, shift_ref, diag_ref, cross_ref, means, armate, stz, sty, off, offin, left, right,
     grams, mates, sums, ylow, yhigh, yfirst, ylast, ynext, yprev, zsend, zgot,
     s_in, s_core, r_core, s_z, r_z, s_y, r_y, s_zb, r_zb, s_cb, r_cb,
-    s_m, r_m, s_x, r_x, s_c, r_c, s_y1, r_y1, s_y2, r_y2, s_zz, r_zz, s_h, r_h,
+    s_m, r_m, s_x, r_x, s_c, r_c, s_y1, r_y1, s_y2, r_y2, s_zz, r_zz, s_out,
     s_s1, r_s1, s_sz, r_sz, s_sy, r_sy, s_g, r_g,
 ):
     y, z, core = place()
@@ -98,12 +98,24 @@
     mate = at(y, z, 1 - core)
     north, south = lax.rem(y + 1, NY), lax.rem(y + NY - 1, NY)
     far = lax.rem(y + 2, NY)
-    ready = greet(plane_peers(y, z, core) + [pair])
+    beyond = lax.axis_index("head") + 1 - 2 * parity
+
+    def across(to):
+        return {**at(y, to, core), "head": beyond}
+
+    ready = greet(
+        plane_peers(y, z, core) + [across(lax.rem(z + i, NZ)) for i in range(NZ)]
+    )
     out = []
 
     def keep(copy):
         out.append(copy)
         return copy
+
+    def batch(ref, sem):
+        return pltpu.make_async_remote_copy(
+            src_ref=ref, dst_ref=ref, send_sem=sem, recv_sem=sem, device_id=mate, device_id_type=MESH
+        )
 
     def load(src, dst, sem):
         copy = pltpu.make_async_copy(src, dst, sem)
@@ -130,8 +142,12 @@
         step *= 2
     cum[...] = total
     turned = jnp.transpose(total)
-    for head in range(8):
-        col[head] = jnp.broadcast_to(turned[:, head : head + 1], (4 * SPAN, D))
+
+    def columns_of(heads):
+        for head in heads:
+            col[head] = jnp.broadcast_to(turned[:, head : head + 1], (4 * SPAN, D))
+
+    columns_of(range(4))
     part[...] = jnp.zeros_like(part)
 
     def lanes(head):
@@ -215,13 +231,12 @@
         lax.fori_loop(0, NZ, combine, 0)
         for i in range(1, NZ):
             to = lax.rem(z + i, NZ)
-            keep(send(chip.at[g, to], zin.at[g, z], s_z.at[g, i], r_z.at[g, z], at(y, to, core)))
+            send(chip.at[g, to], zin.at[g, z], s_z.at[g], r_z.at[g], at(y, to, core))
+        keep(batch(chip.at[g, pl.ds(0, NZ - 1)], s_z.at[g]))
         zin[g, z] = chip[g, z]
 
     def to_rows(g):
-        for i in range(1, NZ):
-            frm = lax.rem(z + i, NZ)
-            arrived(chip.at[g, frm], zin.at[g, frm], s_z.at[g, i], r_z.at[g, frm], at(y, frm, core))
+        batch(zin.at[g, pl.ds(0, NZ - 1)], r_z.at[g]).wait_recv()
         state, decay = jnp.zeros((PIECE, D), F32), jnp.ones((8, D), F32)
         for j in range(NZ):
             pre[g, j, :PIECE, :] = state
@@ -231,12 +246,11 @@
         yin[g, y, PIECE:, :] = decay
         for i in range(1, NY):
             to = lax.rem(y + i, NY)
-            keep(send(yin.at[g, y], yin.at[g, y], s_y.at[g, i], r_y.at[g, y], at(to, z, core)))
+            send(yin.at[g, y], yin.at[g, y], s_y.at[g], r_y.at[g], at(to, z, core))
+        keep(batch(yin.at[g, pl.ds(0, NY - 1)], s_y.at[g]))
 
     def to_chips(g):
-        for i in range(1, NY):
-            frm = lax.rem(y + i, NY)
-            arrived(yin.at[g, frm], yin.at[g, frm], s_y.at[g, i], r_y.at[g, frm], at(frm, z, core))
+        batch(yin.at[g, pl.ds(0, NY - 1)], r_y.at[g]).wait_recv()
         row = jnp.zeros((PIECE, D), F32)
         for j in range(NY):
             piece = yin[g, j]
@@ -246,15 +260,12 @@
             back[g, j] = expand(piece) * row + piece[:PIECE]
         for i in range(1, NZ):
             to = lax.rem(z + i, NZ)
-            keep(send(back.at[g, to], chipin.at[g, z], s_zb.at[g, i], r_zb.at[g, z], at(y, to, core)))
+            send(back.at[g, to], chipin.at[g, z], s_zb.at[g], r_zb.at[g], at(y, to, core))
+        keep(batch(back.at[g, pl.ds(0, NZ - 1)], s_zb.at[g]))
         chipin[g, z] = back[g, z]
 
     def to_cores(g):
-        for i in range(1, NZ):
-            frm = lax.rem(z + i, NZ)
-            arrived(
-                back.at[g, frm], chipin.at[g, frm], s_zb.at[g, i], r_zb.at[g, frm], at(y, frm, core)
-            )
+        batch(chipin.at[g, pl.ds(0, NZ - 1)], r_zb.at[g]).wait_recv()
 
         def split(owner, carry):
             lead = jnp.where(core == 0, part[g, core, owner], other[g, owner])
@@ -333,14 +344,14 @@
             c_ref.at[other_half, columns(j)], theirs.at[:, columns(j)], s_x.at[j], r_x.at[j], pair
         )
 
-    def to_mate(seg):
-        return keep(send(grams[seg].at[:, 1 - core], mates[seg], s_c.at[seg], r_c.at[seg], mate))
+    targets = (far, north, south, y)
 
     def begin(seg):
         kind, first, wide = SEGMENTS[seg]
         cols = slice(first, first + wide)
-        for i in range(4):
-            rows = slice(i * 256, i * 256 + 256)
+        copies = []
+        for i, target in enumerate(targets):
+            rows = columns(target)
             if kind == DIAG:
                 a, b = c_ref[:, rows], c_ref[:, cols]
             elif kind == CROSS:
@@ -348,59 +359,68 @@
             else:
                 a, b = theirs[:, rows], c_ref[half, cols]
             value = lax.dot_general(a, b, TOK, preferred_element_type=F32)
-            grams[seg][pl.ds(8 * i, 8)] = value.astype(BF16).reshape(8, 2, 16, wide)
-        return to_mate(seg)
+            grams[seg][i] = value.astype(BF16).reshape(NZ, 2, 16, wide)
+            if i in (0, 3):
+                span = pl.ds(0, 1) if i == 0 else pl.ds(1, 3)
+                copies.append(
+                    send(
+                        grams[seg].at[span, :, 1 - core],
+                        mates[seg].at[span],
+                        s_c.at[seg],
+                        r_c.at[seg, i // 3],
+                        mate,
+                    )
+                )
+        keep(batch(mates[seg], s_c.at[seg]))
+        return copies
+
+    def chip_sum(seg, i, which):
+        return grams[seg][i, which, core].astype(F32) + mates[seg][i, which].astype(F32)
 
     def merge(a, b):
         return jnp.concatenate(
             [a[:8] + b[:8], jnp.maximum(a[8:16], b[8:16]), jnp.minimum(a[16:], b[16:])], axis=0
         )
 
-    def add_mate(seg, copy):
-        copy.wait_recv()
-
-        def turn(i, carry):
-            four = pl.ds(i * 4, 4)
-            got = grams[seg][four, core].astype(F32) + mates[seg][four].astype(F32)
-            sums[seg][four] = got.astype(BF16)
-            return carry
-
-        lax.fori_loop(0, NZ, turn, 0)
-        block = sums[seg].at[pl.ds(far * NZ, NZ)]
-        edge = SEGMENTS[seg][2] // 2
-        up = keep(
-            send(block.at[:, :, pl.ds(0, edge)], ylow[seg], s_y1.at[seg, 0], r_y1.at[seg, 0], at(north, z, core))
-        )
-        down = keep(
-            send(block.at[:, :, pl.ds(edge, edge)], yhigh[seg], s_y1.at[seg, 1], r_y1.at[seg, 1], at(south, z, core))
-        )
-        return up, down
-
-    def pass_on(seg, copies):
+    def add_mate(seg, copies):
         copies[0].wait_recv()
-        copies[1].wait_recv()
-        edge = SEGMENTS[seg][2] // 2
 
         def turn(i, carry):
             two = pl.ds(i * 2, 2)
-            a = sums[seg][pl.ds(north * NZ + i * 2, 2)]
-            b = sums[seg][pl.ds(south * NZ + i * 2, 2)]
-            low = a[:, :, :edge].astype(F32) + ylow[seg][two].astype(F32)
-            high = b[:, :, edge:].astype(F32) + yhigh[seg][two].astype(F32)
+            sums[seg][two] = chip_sum(seg, 0, two).astype(BF16)
+            return carry
+
+        lax.fori_loop(0, 4, turn, 0)
+        edge = SEGMENTS[seg][2] // 2
+        send(sums[seg].at[:, :, pl.ds(0, edge)], ylow[seg], s_y1.at[seg], r_y1.at[seg], at(north, z, core))
+        send(sums[seg].at[:, :, pl.ds(edge, edge)], yhigh[seg], s_y1.at[seg], r_y1.at[seg], at(south, z, core))
+        keep(batch(sums[seg], s_y1.at[seg]))
+        return copies[1]
+
+    def pass_on(seg, rest):
+        batch(sums[seg], r_y1.at[seg]).wait_recv()
+        rest.wait_recv()
+        edge = SEGMENTS[seg][2] // 2
+
+        def turn(i, carry):
+            two = pl.ds(i * 2, 2)
+            a = chip_sum(seg, 1, two)
+            b = chip_sum(seg, 2, two)
+            low = a[:, :, :edge] + ylow[seg][two].astype(F32)
+            high = b[:, :, edge:] + yhigh[seg][two].astype(F32)
             ynext[seg][two, :, :edge] = low.astype(BF16)
-            ynext[seg][two, :, edge:] = a[:, :, edge:]
-            yprev[seg][two, :, :edge] = b[:, :, :edge]
+            ynext[seg][two, :, edge:] = a[:, :, edge:].astype(BF16)
+            yprev[seg][two, :, :edge] = b[:, :, :edge].astype(BF16)
             yprev[seg][two, :, edge:] = high.astype(BF16)
             return carry
 
         lax.fori_loop(0, 4, turn, 0)
-        up = keep(send(ynext[seg], yfirst[seg], s_y2.at[seg, 0], r_y2.at[seg, 0], at(north, z, core)))
-        down = keep(send(yprev[seg], ylast[seg], s_y2.at[seg, 1], r_y2.at[seg, 1], at(south, z, core)))
-        return up, down
-
-    def to_z(seg, copies):
-        copies[0].wait_recv()
-        copies[1].wait_recv()
+        send(ynext[seg], yfirst[seg], s_y2.at[seg], r_y2.at[seg], at(north, z, core))
+        send(yprev[seg], ylast[seg], s_y2.at[seg], r_y2.at[seg], at(south, z, core))
+        keep(batch(mates[seg].at[pl.ds(0, 2)], s_y2.at[seg]))
+
+    def to_z(seg):
+        batch(mates[seg].at[pl.ds(0, 2)], r_y2.at[seg]).wait_recv()
         kind, first, wide = SEGMENTS[seg]
         tall = 1024 if kind == TURNED else 0
         start = first + (1024 if kind == CROSS else 0)
@@ -412,22 +432,21 @@
         )
         spread = spread.reshape(NZ, 2, 16, wide) * (1024.0 if kind == DIAG else 512.0)
         spread = jnp.where(core == 0, spread[:, 0], spread[:, 1])
-        got = sums[seg][pl.ds(y * NZ, NZ)].astype(F32) + yfirst[seg][...].astype(F32)
+        got = chip_sum(seg, 3, pl.ds(0, NZ)) + yfirst[seg][...].astype(F32)
         got = got + ylast[seg][...].astype(F32) + spread
         zsend[seg][...] = got.astype(BF16)
-        for i in range(1, NZ):
+        for i in range(0 if kind == TURNED else 1, NZ):
             to = lax.rem(z + i, NZ)
-            keep(
-                send(zsend[seg].at[to], zgot[seg].at[z], s_zz.at[seg, i], r_zz.at[seg, z], at(y, to, core))
-            )
-        zgot[seg][z] = zsend[seg][z]
+            peer = across(to) if kind == TURNED else at(y, to, core)
+            send(zsend[seg].at[to], zgot[seg].at[z], s_zz.at[seg], r_zz.at[seg], peer)
+        count = NZ if kind == TURNED else NZ - 1
+        keep(batch(zsend[seg].at[pl.ds(0, count)], s_zz.at[seg]))
+        if kind != TURNED:
+            zgot[seg][z] = zsend[seg][z]
 
     def from_z(seg):
-        for i in range(1, NZ):
-            frm = lax.rem(z + i, NZ)
-            arrived(
-                zsend[seg].at[frm], zgot[seg].at[frm], s_zz.at[seg, i], r_zz.at[seg, frm], at(y, frm, core)
-            )
+        count = NZ if SEGMENTS[seg][0] == TURNED else NZ - 1
+        batch(zgot[seg].at[pl.ds(0, count)], r_zz.at[seg]).wait_recv()
         got = zgot[seg][0].astype(F32)
         for j in range(1, NZ):
             got = got + zgot[seg][j].astype(F32)
@@ -442,6 +461,7 @@
     ready()
     b0 = to_core(0)
     update(0, core)
+    columns_of(range(4, 8))
     kv_ready(1)
     update(1, 1 - core)
     b1 = to_core(1)
@@ -487,40 +507,40 @@
     stz[z] = merge(st_ref[...], armate[...])
     for i in range(1, NZ):
         to = lax.rem(z + i, NZ)
-        keep(send(stz.at[z], stz.at[z], s_sz.at[i], r_sz.at[z], at(y, to, core)))
+        send(stz.at[z], stz.at[z], s_sz, r_sz, at(y, to, core))
+    keep(batch(stz.at[pl.ds(0, NZ - 1)], s_sz))
     for i in range(1, NY):
         to = lax.rem(y + i, NY)
-        keep(send(means.at[y], means.at[y], s_g.at[i], r_g.at[y], at(to, z, core)))
+        send(means.at[y], means.at[y], s_g, r_g, at(to, z, core))
+    keep(batch(means.at[pl.ds(0, NY - 1)], s_g))
     c1 = begin(1)
     p0 = add_mate(0, c0)
     p1 = add_mate(1, c1)
-    q0 = pass_on(0, p0)
+    pass_on(0, p0)
     from_pair(core)
     from_pair(1 - core)
     c2 = begin(2)
-    q1 = pass_on(1, p1)
-    for i in range(1, NZ):
-        frm = lax.rem(z + i, NZ)
-        arrived(stz.at[frm], stz.at[frm], s_sz.at[i], r_sz.at[frm], at(y, frm, core))
+    pass_on(1, p1)
+    batch(stz.at[pl.ds(0, NZ - 1)], r_sz).wait_recv()
     sty[y] = functools.reduce(merge, [stz[j] for j in range(NZ)])
     for i in range(1, NY):
         to = lax.rem(y + i, NY)
-        keep(send(sty.at[y], sty.at[y], s_sy.at[i], r_sy.at[y], at(to, z, core)))
+        send(sty.at[y], sty.at[y], s_sy, r_sy, at(to, z, core))
+    keep(batch(sty.at[pl.ds(0, NY - 1)], s_sy))
     p2 = add_mate(2, c2)
     from_pair(2)
     c3 = begin(3)
-    for i in range(1, NY):
-        frm = lax.rem(y + i, NY)
-        arrived(means.at[frm], means.at[frm], s_g.at[i], r_g.at[frm], at(frm, z, core))
-        arrived(sty.at[frm], sty.at[frm], s_sy.at[i], r_sy.at[frm], at(frm, z, core))
+    batch(means.at[pl.ds(0, NY - 1)], r_g).wait_recv()
+    batch(sty.at[pl.ds(0, NY - 1)], r_sy).wait_recv()
     every = functools.reduce(merge, [sty[j] for j in range(NY)])
     shift_ref[...] = (every[8:16] + every[16:]) / 2.0
+    writes = [load(shift_ref, shift_hbm, s_out.at[0])]
     off[...] = means[...].reshape(NY * 2, 8, D) - (every[:8] / 64.0)[None]
     offset = keep(send(off, offin, s_m, r_m, pair))
     spread_rows(off, 0)
-    to_z(0, q0)
-    to_z(1, q1)
-    q2 = pass_on(2, p2)
+    to_z(0)
+    to_z(1)
+    pass_on(2, p2)
     p3 = add_mate(3, c3)
     from_pair(3)
     c4 = begin(4)
@@ -528,32 +548,31 @@
     p4 = add_mate(4, c4)
     c6 = begin(6)
     p5 = add_mate(5, c5)
-    q3 = pass_on(3, p3)
+    pass_on(3, p3)
     p6 = add_mate(6, c6)
     offset.wait_recv()
     spread_rows(offin, 1024)
-    to_z(2, q2)
-    q4 = pass_on(4, p4)
-    to_z(3, q3)
-    q5 = pass_on(5, p5)
-    q6 = pass_on(6, p6)
-    diag = jnp.concatenate([from_z(0), from_z(1)], axis=1) / 65536.0
-    to_z(4, q4)
-    to_z(5, q5)
-    to_z(6, q6)
-    cross0 = from_z(2)
-    cross1 = from_z(3)
-    strip[0] = from_z(4)
-    hop0 = keep(send(strip.at[0], hop.at[0], s_h.at[0], r_h.at[0], pair))
-    strip[1] = from_z(5)
-    hop1 = keep(send(strip.at[1], hop.at[1], s_h.at[1], r_h.at[1], pair))
-    cross2 = from_z(6)
-    hop0.wait_recv()
-    hop1.wait_recv()
-    cross = jnp.concatenate([cross0, cross1, cross2], axis=1)
-    cross = (cross + jnp.concatenate([hop[0], hop[1]], axis=1)) / 65536.0
-    cov_ref[:, :1024] = jnp.where(parity == 0, diag, cross)
-    cov_ref[:, 1024:] = jnp.where(parity == 0, cross, diag)
+    to_z(2)
+    pass_on(4, p4)
+    to_z(3)
+    pass_on(5, p5)
+    pass_on(6, p6)
+    diag_ref[...] = jnp.concatenate([from_z(0), from_z(1)], axis=1) / 65536.0
+    block = pl.ds(pl.multiple_of(parity * 1024, 1024), 1024)
+    writes.append(load(diag_ref, cov_hbm.at[:, block], s_out.at[1]))
+    to_z(4)
+    to_z(5)
+    to_z(6)
+    cross_ref[:, :512] = from_z(2)
+    cross_ref[:, 512:768] = from_z(3)
+    cross_ref[:, :512] = (cross_ref[:, :512] + from_z(4)) / 65536.0
+    turned1 = from_z(5)
+    cross_ref[:, 512:768] = (cross_ref[:, 512:768] + turned1[:, :256]) / 65536.0
+    cross_ref[:, 768:] = (from_z(6) + turned1[:, 256:]) / 65536.0
+    block = pl.ds(pl.multiple_of((1 - parity) * 1024, 1024), 1024)
+    writes.append(load(cross_ref, cov_hbm.at[:, block], s_out.at[2]))
+    for copy in writes:
+        copy.wait()
     for copy in out:
         copy.wait_send()
 
@@ -580,7 +599,7 @@
             jax.ShapeDtypeStruct((16, 2048), F32),
         ),
         in_specs=[hbm, hbm, hbm, vm, vm],
-        out_specs=(vm, vm),
+        out_specs=(hbm, hbm),
         scratch_shapes=[
             bf16(count, width),
             bf16(count, width),
@@ -602,8 +621,9 @@
             f32(2, NZ, PIECE, D),
             f32(2, 2, NZ, PIECE, D),
             bf16(512, 1024),
-            f32(2, 16, 512),
-            f32(2, 16, 512),
+            f32(8, D),
+            f32(16, 1024),
+            f32(16, 1024),
             f32(NY, 2, 8, D),
             f32(24, D),
             f32(NZ, 24, D),
@@ -612,9 +632,9 @@
             f32(2 * NY, 8, D),
             bf16(32, 2048),
             bf16(32, 2048),
-            per_segment(32, 2, 16),
-            per_segment(32, 16),
-            per_segment(32, 16),
+            per_segment(NY, NZ, 2, 16),
+            per_segment(NY, NZ, 16),
+            per_segment(NZ, 16),
             per_segment(NZ, 16, share=2),
             per_segment(NZ, 16, share=2),
             per_segment(NZ, 16),
@@ -623,12 +643,11 @@
             per_segment(NZ, 16),
             per_segment(NZ, 16),
             per_segment(NZ, 16),
-            dma((5,)), dma((2,)), dma((2,)), dma((2, NZ)), dma((2, NZ)), dma((2, NY)), dma((2, NY)),
-            dma((2, NZ)), dma((2, NZ)), dma((2,)), dma((2,)),
-            dma, dma, dma((4,)), dma((4,)), dma((SEGS,)), dma((SEGS,)),
-            dma((SEGS, 2)), dma((SEGS, 2)), dma((SEGS, 2)), dma((SEGS, 2)),
-            dma((SEGS, NZ)), dma((SEGS, NZ)), dma((2,)), dma((2,)),
-            dma, dma, dma((NZ,)), dma((NZ,)), dma((NY,)), dma((NY,)), dma((NY,)), dma((NY,)),
+            dma((5,)), dma((2,)), dma((2,)), dma((2,)), dma((2,)), dma((2,)), dma((2,)),
+            dma((2,)), dma((2,)), dma((2,)), dma((2,)),
+            dma, dma, dma((4,)), dma((4,)), dma((SEGS,)), dma((SEGS, 2)),
+            dma((SEGS,)), dma((SEGS,)), dma((SEGS,)), dma((SEGS,)), dma((SEGS,)), dma((SEGS,)), dma((3,)),
+            dma, dma, dma, dma, dma, dma, dma, dma,
         ],
         compiler_params=pltpu.CompilerParams(
             collective_id=0, has_side_effects=True, vmem_limit_bytes=60 * 1024 * 1024

time: 84.4 us -> 79.3 us (0.940); the launches traced: 84.2 us -> 77.8 us
  Pallas kernels: 83.6 us -> 77.1 us
    pallas_call x1, Pallas kernels: 82 us -> 75.6 us  [whole(): pl.pallas_call(kernel, out_shape=(jax.ShapeDtypeStruct((8, D), F32), jax....]
where the time goes in v4:
time: 79.3 us; the launch traced here: 77.8 us
  Pallas kernels  77.1 us (97%)
    pallas_call x1, Pallas kernels, whole(): pl.pallas_call(kernel, out_shape=(jax.ShapeDtypeStruct((8, D), F32), jax....  75.6 us

profile of v4, /device:TPU:1, one launch (start us, length us, event | category | flops | bytes accessed | tf_op | source)
XLA Modules:
  0.0 77.8 jit_solution(15872789788397990824)
XLA Ops:
  0.6 75.6 %whole.1 = (f32[8,128]{1,0:T(8,128)}, f32[16,2048]{1,0:T(8,128)}) custom-call(bf16[1024,1024]{1,0:T(8,128)(2,1)} %q_hbm.1, bf16[1024,1024]{1,0:T(8,128)(2,1)} %k_hbm.1, bf16[1024,1024]{1,0:T(8,128)(2,1)} %v_hbm.1, f32[8,1024]{1,0:T(8,128)} %ld_ref.1, f32[8,128]{1,0:T(8,128)} %bitcast.2), custom_call_target="tpu_custom_call" | custom-call | tf_op jit(solution)/shard_map/whole/pallas_call | solution.py:595
  76.2 1.6 %hand_out.1 = (f32[8,128]{1,0:T(8,128)}, f32[16,2048]{1,0:T(8,128)}) custom-call(f32[8,128]{1,0:T(8,128)} %get-tuple-element.6.a_ref, f32[16,2048]{1,0:T(8,128)} %get-tuple-element.7.b_ref), custom_call_target="tpu_custom_call" | custom-call | tf_op jit(solution)/shard_map/hand_out/pallas_call | solution.py:666

commit v5 on v4

--- a/solution.py
+++ b/solution.py
@@ -546,16 +546,16 @@
     c4 = begin(4)
     c5 = begin(5)
     p4 = add_mate(4, c4)
-    c6 = begin(6)
     p5 = add_mate(5, c5)
     pass_on(3, p3)
+    c6 = begin(6)
     p6 = add_mate(6, c6)
     offset.wait_recv()
     spread_rows(offin, 1024)
     to_z(2)
     pass_on(4, p4)
+    pass_on(5, p5)
     to_z(3)
-    pass_on(5, p5)
     pass_on(6, p6)
     diag_ref[...] = jnp.concatenate([from_z(0), from_z(1)], axis=1) / 65536.0
     block = pl.ds(pl.multiple_of(parity * 1024, 1024), 1024)

time: 79.3 us -> 79.9 us (level); the launches traced: 77.8 us -> 79.7 us
  Pallas kernels: 77.1 us -> 79.1 us
    pallas_call x1, Pallas kernels: 75.6 us -> 77.5 us  [whole(): pl.pallas_call(kernel, out_shape=(jax.ShapeDtypeStruct((8, D), F32), jax....]
where the time goes in v5:
time: 79.9 us; the launch traced here: 79.7 us
  Pallas kernels  79.1 us (99%)
    pallas_call x1, Pallas kernels, whole(): pl.pallas_call(kernel, out_shape=(jax.ShapeDtypeStruct((8, D), F32), jax....  77.5 us

profile of v5, /device:TPU:1, one launch (start us, length us, event | category | flops | bytes accessed | tf_op | source)
XLA Modules:
  0.0 79.7 jit_solution(8562662955793119012)
XLA Ops:
  0.6 77.5 %whole.1 = (f32[8,128]{1,0:T(8,128)}, f32[16,2048]{1,0:T(8,128)}) custom-call(bf16[1024,1024]{1,0:T(8,128)(2,1)} %q_hbm.1, bf16[1024,1024]{1,0:T(8,128)(2,1)} %k_hbm.1, bf16[1024,1024]{1,0:T(8,128)(2,1)} %v_hbm.1, f32[8,1024]{1,0:T(8,128)} %ld_ref.1, f32[8,128]{1,0:T(8,128)} %bitcast.2), custom_call_target="tpu_custom_call" | custom-call | tf_op jit(solution)/shard_map/whole/pallas_call | solution.py:595
  78.1 1.6 %hand_out.1 = (f32[8,128]{1,0:T(8,128)}, f32[16,2048]{1,0:T(8,128)}) custom-call(f32[8,128]{1,0:T(8,128)} %get-tuple-element.6.a_ref, f32[16,2048]{1,0:T(8,128)} %get-tuple-element.7.b_ref), custom_call_target="tpu_custom_call" | custom-call | tf_op jit(solution)/shard_map/hand_out/pallas_call | solution.py:666
